TPU v7x, 256 devices: a whole 4x4x8 slice. The times are simulated.
256 devices in a mesh: blk: 16 (over y_lo, z), section: 8 (over x, core), tp: 2 (over y_hi).
Axes of the slice: x: 4, y: 4 (y_hi: 2, y_lo: 2; y = y_hi * 2 + y_lo), z: 8, core: 2. Of those that a mesh axis runs over, the one named last changes fastest.
Arguments:
- queries: bfloat16 [16384, 1280], P('blk', ('section', 'tp')), may hold values from -180 to 180
- keys: bfloat16 [16384, 1280], P('blk', ('section', 'tp')), may hold values from -6 to 6
- values: bfloat16 [16384, 1280], P('blk', ('section', 'tp')), may hold values from -6 to 6
- segment_ids: int32 [16384], P('blk'), may hold values from 0 to 7, never falling along the last dimension, each value on 1 to 9216 neighbouring positions
- out_weight: bfloat16 [1280, 1280], P(('section', 'tp')), may hold values from -0.15625 to 0.15625
- norm_gain: float32 [1280], replicated, may hold values from 0.1 to 1.9
- norm_bias: float32 [1280], replicated, may hold values from -3 to 3
- proj_weight: bfloat16 [5120, 5120], P(None, ('section', 'tp')), may hold values from -0.078125 to 0.078125
- proj_bias: float32 [5120], P(('section', 'tp')), may hold values from -3 to 3
Outputs:
- projected: bfloat16 [4096, 5120], P('blk', ('section', 'tp'))
Inputs may be any that keep to these rules, and one draw needn't show every extreme that they name: `segment_ids`: image numbers never fall along the patch order, so each image covers consecutive patches; one image covers exactly 9216 patches.
All inputs are finite; a program needn't handle non-finite values.
Results may differ from a plain program's by a relative error of at most 0.02.
Values may be sent and summed in bfloat16 or wider, within the bound.
No kernel may reach another device: no remote copies, remote signals or barrier semaphores. Data moves between devices by JAX's collectives and lax.ppermute only.
A program may use at most 64 MiB of HBM per device.

v0:
```python
import functools

import jax
import jax.numpy as jnp
from jax import lax
from jax.experimental import pallas as pl
from jax.experimental.pallas import tpu as pltpu
from jax.sharding import PartitionSpec as P

HDIM = 80
EPSILON = 1e-06
EXP2_SCALE = 1.4426950408889634 * HDIM ** (-0.5)
MASKED = -1e30
NO_MAX = -1e20
MOST_EXCESS = 60.0 / EXP2_SCALE
KEY_PARTNERS = (0, 1, 8, 9)
QUERY_PARTNERS = (0, 4, 10, 14)
f32, bf16 = jnp.float32, jnp.bfloat16
GROUP = ("section", "tp")
IN_VMEM = pl.BlockSpec(memory_space=pltpu.VMEM)
IN_SMEM = pl.BlockSpec(memory_space=pltpu.SMEM)


def pack_kernel(queries, keys, values, ids, query_block, key_block, held_ids, sems):
    count = queries.shape[1]
    moves = [
        (ids, held_ids),
        (queries, query_block.at[0:80, :]),
        (keys, key_block.at[0:80, :]),
        (values, key_block.at[80:160, :]),
    ]
    copies = [pltpu.make_async_copy(*move, sems.at[i]) for i, move in enumerate(moves)]
    for copy in copies:
        copy.start()
    copies[0].wait()
    id_row = held_ids[...].astype(f32)
    zeros = jnp.zeros((6, count), f32)
    query_block[80:88, :] = jnp.concatenate([id_row, id_row, zeros], axis=0).astype(bf16)
    key_block[160:168, :] = jnp.concatenate([jnp.ones_like(id_row), id_row, zeros], axis=0).astype(bf16)
    for copy in copies[1:]:
        copy.wait()


def pack(queries, keys, values, ids):
    count = queries.shape[1]
    return pl.pallas_call(
        pack_kernel,
        out_shape=[
            jax.ShapeDtypeStruct((88, count), bf16),
            jax.ShapeDtypeStruct((168, count), bf16),
        ],
        in_specs=[pl.BlockSpec(memory_space=pltpu.HBM)] * 4,
        out_specs=[IN_VMEM] * 2,
        scratch_shapes=[pltpu.VMEM((1, count), jnp.int32), pltpu.SemaphoreType.DMA((4,))],
        compiler_params=pltpu.CompilerParams(vmem_limit_bytes=4 << 20),
        name="pack",
    )(*(pltpu.with_memory_space_constraint(x, pltpu.HBM) for x in (queries, keys, values, ids)))


def attend_block(query, held_k, held_v, limits, which, row_max, total, excess):
    count = query.shape[1]
    tiles, sub = 2, 256
    q_low, q_high = limits[which, 0], limits[which, 3]

    def tile(kb, start, tile_keys, masked, raising):
        rows = pl.ds(start, tile_keys)
        key_tile = held_k[kb, rows, :]
        value_tile = held_v[kb, :, rows]
        if masked:
            key_ids = jnp.broadcast_to(value_tile[80:88, :].T.astype(f32)[:, 1:2], (tile_keys, sub))

        def score(j):
            columns = slice(j * sub, (j + 1) * sub)
            found = jnp.dot(key_tile, query[0:80, columns], preferred_element_type=f32)
            if masked:
                query_ids = query[80:88, columns].astype(f32)[0:1, :]
                found = jnp.where(key_ids == query_ids, found, MASKED)
            return found

        scores = score(0)
        for j in range(count // sub):
            following = score(j + 1) if (j + 1) * sub < count else None
            columns = slice(j * sub, (j + 1) * sub)
            old = row_max[:, columns]
            if raising:
                new = jnp.maximum(old, jnp.max(scores, axis=0, keepdims=True))
                weights = jnp.exp2((scores - new) * EXP2_SCALE).astype(bf16)
                rescale = jnp.exp2((old - new) * EXP2_SCALE)
                total[:, columns] = total[:, columns] * rescale + jnp.dot(
                    value_tile, weights, preferred_element_type=f32
                )
                row_max[:, columns] = new
            else:
                weights = jnp.exp2((scores - old) * EXP2_SCALE).astype(bf16)
                total[:, columns] = total[:, columns] + jnp.dot(
                    value_tile, weights, preferred_element_type=f32
                )
                above = jnp.max(scores, axis=0, keepdims=True) - old
                excess[:, columns] = jnp.maximum(excess[:, columns], above)
            scores = following

    def every_key_block(keep_shift):
        row_max[...] = jnp.full_like(row_max, NO_MAX)
        total[...] = jnp.zeros_like(total)
        excess[...] = jnp.zeros_like(excess)

        def key_block_step(kb, started):
            low, high = limits[4 + kb, 0], limits[4 + kb, 3]
            whole = jnp.logical_and(jnp.logical_and(low == high, q_low == q_high), low == q_low)
            still = jnp.logical_and(jnp.logical_and(whole, started > 0), keep_shift)

            @pl.when(still)
            def _():
                tile(kb, 0, count, False, False)

            @pl.when(jnp.logical_and(whole, jnp.logical_not(still)))
            def _():
                tile(kb, 0, count, False, True)

            @pl.when(jnp.logical_not(whole))
            def _():
                def half(t, unused):
                    low, high = limits[4 + kb, 2 * t], limits[4 + kb, 2 * t + 1]

                    @pl.when(jnp.logical_and(low <= q_high, high >= q_low))
                    def _():
                        tile(kb, pl.multiple_of(t * (count // tiles), 128), count // tiles, True, True)

                    return 0

                lax.fori_loop(0, tiles, half, 0)

            return jnp.maximum(started, whole.astype(jnp.int32))

        lax.fori_loop(0, 4, key_block_step, 0)

    def attempt(tried, unused):
        @pl.when(jnp.logical_or(tried == 0, jnp.max(excess[...]) > MOST_EXCESS))
        def _():
            every_key_block(tried == 0)

        return 0

    lax.fori_loop(0, 2, attempt, 0)


def store_partial(out, row_max, total):
    def split(value, parts):
        pieces = []
        for _ in range(parts):
            piece = value.astype(bf16).astype(f32)
            pieces.append(piece)
            value = value - piece
        return pieces

    rows = split(total[80:81, :], 2) + split(row_max[...], 3)
    rows.append(jnp.zeros((3, out.shape[1]), f32))
    out[0:80, :] = total[0:80, :].astype(bf16)
    out[80:88, :] = jnp.concatenate(rows, axis=0).astype(bf16)


def copy_limits(limits, limits_s, sem):
    copy = pltpu.make_async_copy(limits, limits_s, sem)
    copy.start()
    copy.wait()


def attend_first_kernel(blocks, *refs):
    queries, key_values = refs[0:4], refs[4:8]
    outs = refs[8 : 8 + len(blocks)]
    (held_k, held_v, limits, query, ids, limits_s, row_max, total, excess, sem) = refs[8 + len(blocks) :]
    count = queries[0].shape[1]
    for i in range(4):
        held_k[i] = key_values[i][0:80, :].T
        held_v[i] = key_values[i][80:168, :]
        ids[i : i + 1, :] = queries[i][80:88, :].astype(f32)[0:1, :]
        ids[4 + i : 5 + i, :] = key_values[i][160:168, :].astype(f32)[1:2, :]
    lane = lax.broadcasted_iota(jnp.int32, (8, 128), 1)
    table = jnp.zeros((8, 128), f32)
    for t in range(2):
        part = ids[:, t * (count // 2) : (t + 1) * (count // 2)]
        table = jnp.where(lane == 2 * t, jnp.min(part, axis=1, keepdims=True), table)
        table = jnp.where(lane == 2 * t + 1, jnp.max(part, axis=1, keepdims=True), table)
    limits[...] = table.astype(jnp.int32)
    copy_limits(limits, limits_s, sem)
    for i, block in enumerate(blocks):
        query[i] = queries[block][...]

    def one(i, unused):
        attend_block(query.at[i], held_k, held_v, limits_s, blocks[0] + i, row_max, total, excess)
        for o in range(len(blocks)):

            @pl.when(i == o)
            def _():
                store_partial(outs[o], row_max, total)

        return 0

    lax.fori_loop(0, len(blocks), one, 0)


def attend_first(queries, key_values, blocks):
    count = queries[0].shape[1]
    return pl.pallas_call(
        functools.partial(attend_first_kernel, blocks),
        out_shape=[jax.ShapeDtypeStruct((88, count), bf16)] * len(blocks)
        + [
            jax.ShapeDtypeStruct((4, count, 80), bf16),
            jax.ShapeDtypeStruct((4, 88, count), bf16),
            jax.ShapeDtypeStruct((8, 128), jnp.int32),
        ],
        in_specs=[IN_VMEM] * 8,
        out_specs=[IN_VMEM] * (3 + len(blocks)),
        scratch_shapes=[
            pltpu.VMEM((len(blocks), 88, count), bf16),
            pltpu.VMEM((8, count), f32),
            pltpu.SMEM((8, 128), jnp.int32),
            pltpu.VMEM((1, count), f32),
            pltpu.VMEM((88, count), f32),
            pltpu.VMEM((1, count), f32),
            pltpu.SemaphoreType.DMA,
        ],
        compiler_params=pltpu.CompilerParams(vmem_limit_bytes=16 << 20),
        name="attend_first",
    )(*queries, *key_values)


def attend_next_kernel(
    block, query, held_k, held_v, limits, out, limits_s, row_max, total, excess, sem
):
    copy_limits(limits, limits_s, sem)
    attend_block(query, held_k, held_v, limits_s, block, row_max, total, excess)
    store_partial(out, row_max, total)


def attend_next(block, query, held_k, held_v, limits):
    count = query.shape[1]
    return pl.pallas_call(
        functools.partial(attend_next_kernel, block),
        out_shape=jax.ShapeDtypeStruct((88, count), bf16),
        in_specs=[IN_VMEM] * 4,
        out_specs=IN_VMEM,
        scratch_shapes=[
            pltpu.SMEM((8, 128), jnp.int32),
            pltpu.VMEM((1, count), f32),
            pltpu.VMEM((88, count), f32),
            pltpu.VMEM((1, count), f32),
            pltpu.SemaphoreType.DMA,
        ],
        compiler_params=pltpu.CompilerParams(vmem_limit_bytes=12 << 20),
        name="attend_next",
    )(query, held_k, held_v, limits)


def combine_kernel(*refs):
    parts, out = refs[:4], refs[4]
    sums, maxima = [], []
    for part in parts:
        rows = part[80:88, :].astype(f32)
        sums.append(rows[0:1, :] + rows[1:2, :])
        maxima.append((rows[2:3, :] + rows[3:4, :]) + rows[4:5, :])
    top = functools.reduce(jnp.maximum, maxima)
    factors = [jnp.exp2((m - top) * EXP2_SCALE) for m in maxima]
    whole = functools.reduce(jnp.add, [w * s for w, s in zip(factors, sums)])
    inverse = 1.0 / whole
    mixed = functools.reduce(
        jnp.add, [part[0:80, :].astype(f32) * w for part, w in zip(parts, factors)]
    )
    out[...] = (mixed * inverse).astype(bf16)


def combine(parts):
    count = parts[0].shape[1]
    return pl.pallas_call(
        combine_kernel,
        out_shape=jax.ShapeDtypeStruct((80, count), bf16),
        in_specs=[IN_VMEM] * 4,
        out_specs=IN_VMEM,
        compiler_params=pltpu.CompilerParams(vmem_limit_bytes=6 << 20),
        name="combine",
    )(*parts)


def place_heads(heads, at, pieces, whole, sems):
    copies = []
    for piece in pieces:
        for i in range(piece.shape[0] // HDIM):
            row = pl.multiple_of(heads[at + len(copies)] * HDIM, 16)
            source = piece if piece.shape[0] == HDIM else piece.at[pl.ds(i * HDIM, HDIM), :]
            copy = pltpu.make_async_copy(source, whole.at[pl.ds(row, HDIM), :], sems.at[len(copies)])
            copy.start()
            copies.append(copy)
    return copies


def assemble_kernel(heads, *refs):
    pieces, whole, sems = refs[:-2], refs[-2], refs[-1]
    for copy in place_heads(heads, 16, pieces, whole, sems):
        copy.wait()


def assemble(heads, pieces):
    return pl.pallas_call(
        assemble_kernel,
        out_shape=jax.ShapeDtypeStruct((8 * HDIM, pieces[0].shape[1]), bf16),
        in_specs=[IN_SMEM] + [pl.BlockSpec(memory_space=pl.ANY)] * len(pieces),
        out_specs=IN_VMEM,
        scratch_shapes=[pltpu.SemaphoreType.DMA((8,))],
        compiler_params=pltpu.CompilerParams(vmem_limit_bytes=5 << 20),
        name="assemble",
    )(heads, *pieces)


def join_kernel(*refs):
    halves, whole, sems = refs[:-2], refs[-2], refs[-1]
    rows = halves[0].shape[0]
    copies = [
        pltpu.make_async_copy(half, whole.at[pl.ds(i * rows, rows), :], sems.at[i])
        for i, half in enumerate(halves)
    ]
    for copy in copies:
        copy.start()
    for copy in copies:
        copy.wait()


def join(halves):
    rows, width = halves[0].shape
    return pl.pallas_call(
        join_kernel,
        out_shape=jax.ShapeDtypeStruct((len(halves) * rows, width), bf16),
        in_specs=[pl.BlockSpec(memory_space=pl.ANY)] * len(halves),
        out_specs=IN_VMEM,
        scratch_shapes=[pltpu.SemaphoreType.DMA((len(halves),))],
        compiler_params=pltpu.CompilerParams(vmem_limit_bytes=5 << 20),
        name="join",
    )(*halves)


def project_kernel(count, heads, *refs):
    pieces = refs[:10]
    (weight, gain, shift, proj, proj_bias, out, attended, normed, sems) = refs[10:]
    copies = place_heads(heads, 0, pieces, attended, sems)
    width = weight.shape[1]
    step = 512
    bias_column = jnp.broadcast_to(proj_bias[...], (8, proj.shape[0])).T[:, 0:1]
    for copy in copies:
        copy.wait()
    for b in range(count // step):
        turned = attended[:, b * step : (b + 1) * step].T
        rows = jnp.dot(turned, weight[...], preferred_element_type=f32).astype(bf16).astype(f32)
        rows = rows - jnp.sum(rows, axis=1, keepdims=True) * (1.0 / width)
        spread = jnp.sum(rows * rows, axis=1, keepdims=True) * (1.0 / width)
        rows = rows * lax.rsqrt(spread + EPSILON) * gain[...] + shift[...]
        for k in range(width // 128):
            normed[b, k] = rows[:, k * 128 : (k + 1) * 128]
        linear = jnp.zeros((proj.shape[0], step // 4), f32)
        for r in range(4):
            every_fourth = pl.ds(r, step // 4, stride=4)
            tokens = jnp.concatenate(
                [normed[b, k, every_fourth, :].astype(bf16) for k in range(width // 128)], axis=1
            )
            linear = linear + lax.dot_general(
                proj[:, r * width : (r + 1) * width],
                tokens,
                (((1,), (1,)), ((), ())),
                preferred_element_type=f32,
            )
        linear = linear + bias_column
        active = 0.5 * linear * (1.0 + lax.erf(linear * (0.5**0.5)))
        out[:, b * (step // 4) : (b + 1) * (step // 4)] = active.astype(bf16)


def project(heads, pieces, weight, gain, shift, proj, proj_bias):
    count = pieces[0].shape[1]
    depth, width = weight.shape
    return pl.pallas_call(
        functools.partial(project_kernel, count),
        out_shape=jax.ShapeDtypeStruct((proj.shape[0], count // 4), bf16),
        in_specs=[IN_SMEM] + [pl.BlockSpec(memory_space=pl.ANY)] * 10 + [IN_VMEM] * 5,
        out_specs=IN_VMEM,
        scratch_shapes=[
            pltpu.VMEM((depth, count), bf16),
            pltpu.VMEM((count // 512, width // 128, 512, 128), f32),
            pltpu.SemaphoreType.DMA((16,)),
        ],
        compiler_params=pltpu.CompilerParams(vmem_limit_bytes=30 << 20),
        name="project",
    )(heads, *pieces, weight, gain, shift, proj, proj_bias)


def head_order():
    table = []
    for x in range(4):
        for c in range(2):
            for t in range(2):

                def slot(a, d, b):
                    return (d != c) * 8 + a % 4 * 2 + b

                row = [slot(x, c, t), slot(x, 1 - c, t)]
                for d in (c, 1 - c):
                    side = x + (3, 1)[d]
                    cross = (x + 2, t) if d == 0 else (x, 1 - t)
                    row += [slot(side, d, t), slot(side, 1 - d, t)]
                    row += [slot(cross[0], d, cross[1]), slot(cross[0], 1 - d, cross[1])]
                    row += [slot(side, d, 1 - t), slot(side, 1 - d, 1 - t)]
                    row += [slot(x + 2, d, 1 - t)]
                for a in (x, x + 3, x + 1, x + 2):
                    row += [slot(a, c, t), slot(a, c, 1 - t)]
                table.append(row)
    return table


def on_device(
    queries, keys, values, segment_ids, out_weight, norm_gain, norm_bias, proj_weight, proj_bias
):
    blocks = lax.axis_size("blk")
    query_block, key_block = pack(queries.T, keys.T, values.T, segment_ids[None, :])

    sections = lax.axis_size("section")

    def swap(block, mask):
        if mask == 0:
            return block
        perm = []
        for i in range(blocks):
            for section in range(sections):
                turn = section % 2
                y, z = i // 8 ^ mask >> 3, ((i % 8 - turn) % 8 ^ mask & 7) + turn
                perm.append((i * sections + section, (y * 8 + z % 8) * sections + section))
        return lax.ppermute(block, ("blk", "section"), perm)

    def send(block, to):
        perm = []
        for x in range(4):
            for c in range(2):
                for t in range(2):
                    a, b, d = to(x, c, t)
                    perm.append(((x * 2 + c) * 2 + t, (a % 4 * 2 + b) * 2 + d))
        return lax.ppermute(block, GROUP, perm)

    far = send(out_weight, lambda x, c, t: (x, c, 1 - t))
    me = lax.axis_index("section") * 2 + lax.axis_index("tp")
    heads = jnp.asarray(head_order(), jnp.int32)[me]

    def across(x, c, t):
        return x, 1 - c, t

    key_blocks = [swap(key_block, mask) for mask in KEY_PARTNERS]
    query_blocks = [swap(query_block, mask) for mask in QUERY_PARTNERS]
    both = jnp.concatenate([out_weight, far], axis=0)
    both, query_blocks, key_blocks = lax.optimization_barrier((both, query_blocks, key_blocks))
    weights = [both] + [send(both, lambda x, c, t, d=d: (x + d, c, t)) for d in (1, 3, 2)]
    *partial, held_k, held_v, limits = attend_first(query_blocks, key_blocks, (1, 2, 3))
    returned = [swap(part, mask) for part, mask in zip(partial, QUERY_PARTNERS[1:])]
    own_query, partial = lax.optimization_barrier((query_blocks[0], partial))
    returned.append(attend_next(0, own_query, held_k, held_v, limits))
    weights, returned[3] = lax.optimization_barrier((weights, returned[3]))
    half = assemble(heads, weights)
    returned, half = lax.optimization_barrier((returned, half))
    other_half = send(half, across)
    attended = combine(returned)

    def along(x, c, t):
        return x + (1, -1)[c], c, t

    def along_far(x, c, t):
        return x + (1, -1)[c], c, 1 - t

    def opposite(x, c, t):
        return (x + 2, c, t) if c == 0 else (x, c, 1 - t)

    def opposite_far(x, c, t):
        return x + 2, c, 1 - t

    sibling = send(attended, across)
    pair = jnp.concatenate([attended, sibling], axis=0)
    received = [send(pair, along), send(pair, opposite), send(pair, along_far)]
    received.append(send(attended, opposite_far))
    weight, received[-1] = lax.optimization_barrier((join([half, other_half]), received[-1]))
    forwarded = [send(block, across) for block in received]
    pieces = [attended, sibling] + received + forwarded
    projected = project(
        heads,
        pieces,
        weight,
        norm_gain[None, :],
        norm_bias[None, :],
        proj_weight.T,
        proj_bias[None, :],
    )
    return projected.T


def solution(mesh):
    placed = (
        P("blk", GROUP),
        P("blk", GROUP),
        P("blk", GROUP),
        P("blk"),
        P(GROUP, None),
        P(),
        P(),
        P(None, GROUP),
        P(GROUP),
    )
    return jax.shard_map(
        on_device,
        mesh=mesh,
        in_specs=placed,
        out_specs=P("blk", GROUP),
        check_vma=False,
    )
```

profile of v0, /device:TPU:1, one launch (start us, length us, event | category | flops | bytes accessed | tf_op | source)
XLA Modules:
  0.0 116.1 jit_solution(1254290051940877712)
XLA Ops:
  0.0 3.7 %collective-permute-start = (bf16[80,1280]{1,0:T(8,128)(2,1)}, bf16[80,1280]{1,0:T(8,128)(2,1)S(1)}, u32[]{:S(2)}, u32[]{:S(2)}) collective-permute-start(bf16[80,1280]{1,0:T(8,128)(2,1)} %param.14), channel_id=1, source_target_pairs={{0,1},{1,0},{2,3},{3,2},{4,5},{5,4},{6,7},{7,6},{8,9},{9,8},{10,11... | collective-permute-start | bytes 614408 | tf_op jit(solution)/shard_map/ppermute | solution.py:441
  3.7 1.1 pack.1
  4.9 7.0 %collective-permute-start.1 = (bf16[88,1024]{1,0:T(8,128)(2,1)S(1)}, bf16[88,1024]{1,0:T(8,128)(2,1)S(1)}, u32[]{:S(2)}, u32[]{:S(2)}) collective-permute-start(bf16[88,1024]{1,0:T(8,128)(2,1)S(1)} %get-tuple-element.49.refs_0_.query), channel_id=1, source_target_pairs={{0,64},{2,66},{4,68},{6,70},{8,72},{10,74},{12,76},{14,78},{16,80}... | collective-permute-start | bytes 540680 | tf_op jit(solution)/shard_map/ppermute | solution.py:432
  11.9 0.0 collective-permute-start.4
  11.9 0.4 collective-permute-start.5
  12.3 3.5 %collective-permute-start.6 = (bf16[168,1024]{1,0:T(8,128)(2,1)S(1)}, bf16[168,1024]{1,0:T(8,128)(2,1)S(1)}, u32[]{:S(2)}, u32[]{:S(2)}) collective-permute-start(bf16[168,1024]{1,0:T(8,128)(2,1)S(1)} %get-tuple-element.41.refs_4_), channel_id=1, source_target_pairs={{0,144},{2,242},{4,148},{6,246},{8,152},{10,250},{12,156},{14,254}... | collective-permute-start | bytes 1032200 | tf_op jit(solution)/shard_map/ppermute | solution.py:432
  15.7 0.1 collective-permute-done.1.refs_1_
  15.9 8.6 %collective-permute-start.2 = (bf16[88,1024]{1,0:T(8,128)(2,1)S(1)}, bf16[88,1024]{1,0:T(8,128)(2,1)S(1)}, u32[]{:S(2)}, u32[]{:S(2)}) collective-permute-start(bf16[88,1024]{1,0:T(8,128)(2,1)S(1)} %get-tuple-element.49.refs_0_.query), channel_id=1, source_target_pairs={{0,160},{2,226},{4,164},{6,230},{8,168},{10,234},{12,172},{14,238}... | collective-permute-start | bytes 540680 | tf_op jit(solution)/shard_map/ppermute | solution.py:432
  24.4 0.0 collective-permute-done
  24.4 0.0 collective-permute-start.3
  24.4 1.0 pad_maximum_fusion.refs_0_
  25.4 7.3 %collective-permute-done.2.refs_2_ = bf16[88,1024]{1,0:T(8,128)(2,1)S(1)} collective-permute-done((bf16[88,1024]{1,0:T(8,128)(2,1)S(1)}, bf16[88,1024]{1,0:T(8,128)(2,1)S(1)}, u32[]{:S(2)}, u32[]{:S(2)}) %collective-permute-start.2) | collective-permute-done | bytes 180256 | tf_op jit(solution)/shard_map/ppermute | solution.py:432
  32.7 4.6 %collective-permute-done.3.refs_3_ = bf16[88,1024]{1,0:T(8,128)(2,1)S(1)} collective-permute-done((bf16[88,1024]{1,0:T(8,128)(2,1)S(1)}, bf16[88,1024]{1,0:T(8,128)(2,1)S(1)}, u32[]{:S(2)}, u32[]{:S(2)}) %collective-permute-start.3) | collective-permute-done | bytes 180256 | tf_op jit(solution)/shard_map/ppermute | solution.py:432
  37.3 0.0 collective-permute-done.4.refs_5_
  37.3 0.0 collective-permute-done.5.refs_6_
  37.3 0.0 collective-permute-done.6.refs_7_
  37.3 1.3 %collective-permute-start.10 = (bf16[160,1280]{1,0:T(8,128)(2,1)S(1)}, bf16[160,1280]{1,0:T(8,128)(2,1)S(1)}, u32[]{:S(2)}, u32[]{:S(2)}) collective-permute-start(bf16[160,1280]{1,0:T(8,128)(2,1)S(1)} %pad_maximum_fusion.refs_0_), channel_id=1, source_target_pairs={{0,4},{1,5},{2,6},{3,7},{4,8},{5,9},{6,10},{7,11},{8,12},{9,13},{1... | collective-permute-start | bytes 1228808 | tf_op jit(solution)/shard_map/ppermute | solution.py:441
  38.6 1.5 %collective-permute-start.11 = (bf16[160,1280]{1,0:T(8,128)(2,1)S(1)}, bf16[160,1280]{1,0:T(8,128)(2,1)S(1)}, u32[]{:S(2)}, u32[]{:S(2)}) collective-permute-start(bf16[160,1280]{1,0:T(8,128)(2,1)S(1)} %pad_maximum_fusion.refs_0_), channel_id=1, source_target_pairs={{0,12},{1,13},{2,14},{3,15},{4,0},{5,1},{6,2},{7,3},{8,4},{9,5},{1... | collective-permute-start | bytes 1228808 | tf_op jit(solution)/shard_map/ppermute | solution.py:441
  40.0 1.5 %collective-permute-start.12 = (bf16[160,1280]{1,0:T(8,128)(2,1)S(1)}, bf16[160,1280]{1,0:T(8,128)(2,1)}, u32[]{:S(2)}, u32[]{:S(2)}) collective-permute-start(bf16[160,1280]{1,0:T(8,128)(2,1)S(1)} %pad_maximum_fusion.refs_0_), channel_id=1, source_target_pairs={{0,8},{1,9},{2,10},{3,11},{4,12},{5,13},{6,14},{7,15},{8,0},{9,1},... | collective-permute-start | bytes 1228808 | tf_op jit(solution)/shard_map/ppermute | solution.py:441
  41.6 9.6 %attend_first.1 = (bf16[88,1024]{1,0:T(8,128)(2,1)}, bf16[88,1024]{1,0:T(8,128)(2,1)}, bf16[88,1024]{1,0:T(8,128)(2,1)}, bf16[4,1024,80]{2,1,0:T(8,128)(2,1)S(1)...) custom-call(bf16[88,1024]{1,0:T(8,128)(2,1)S(1)} %get-tuple-element.49.refs_0_.query, ...), custom_call_target="tpu_custom_call" | custom-call | tf_op jit(solution)/shard_map/attend_first/pallas_call | solution.py:204
  51.2 4.4 %collective-permute-start.7 = (bf16[88,1024]{1,0:T(8,128)(2,1)}, bf16[88,1024]{1,0:T(8,128)(2,1)S(1)}, u32[]{:S(2)}, u32[]{:S(2)}) collective-permute-start(bf16[88,1024]{1,0:T(8,128)(2,1)} %get-tuple-element.45), channel_id=1, source_target_pairs={{0,64},{2,66},{4,68},{6,70},{8,72},{10,74},{12,76},{14,78},{16,80}... | collective-permute-start | bytes 540680 | tf_op jit(solution)/shard_map/ppermute | solution.py:432
  55.6 3.9 %collective-permute-start.8 = (bf16[88,1024]{1,0:T(8,128)(2,1)}, bf16[88,1024]{1,0:T(8,128)(2,1)S(1)}, u32[]{:S(2)}, u32[]{:S(2)}) collective-permute-start(bf16[88,1024]{1,0:T(8,128)(2,1)} %get-tuple-element.46), channel_id=1, source_target_pairs={{0,160},{2,226},{4,164},{6,230},{8,168},{10,234},{12,172},{14,238}... | collective-permute-start | bytes 540680 | tf_op jit(solution)/shard_map/ppermute | solution.py:432
  59.5 0.0 collective-permute-done.10.refs_1_
  59.5 0.0 collective-permute-start.9
  59.5 0.7 dynamic-slice_bitcast_fusion.heads
  60.2 5.3 %attend_next.1.refs_3_ = bf16[88,1024]{1,0:T(8,128)(2,1)S(1)} custom-call(bf16[88,1024]{1,0:T(8,128)(2,1)S(1)} %get-tuple-element.49.refs_0_.query, bf16[4,1024,80]{2,1,0:T(8,128)(2,1)S(1)} %get-tuple-element.50.held_k, bf16[4,88,1024]{2,1,0:T(8,128)(2,1)S(1)} %get-tuple-element.51.held_v, s32[8,128]{1,0:T(8,128)S(1)} %get-tuple-element.52.limits), custom_call_target="tpu_custom_call" | custom-call | tf_op jit(solution)/shard_map/attend_next/pallas_call | solution.py:238
  65.4 0.0 collective-permute-done.11.refs_2_
  65.5 0.0 collective-permute-done.12.refs_3_
  65.5 3.3 %assemble.1.refs_0_ = bf16[640,1280]{1,0:T(8,128)(2,1)S(1)} custom-call(s32[24]{0:T(128)S(1)} %dynamic-slice_bitcast_fusion.heads, bf16[160,1280]{1,0:T(8,128)(2,1)S(1)} %pad_maximum_fusion.refs_0_, bf16[160,1280]{1,0:T(8,128)(2,1)S(1)} %collective-permute-done.10.refs_1_, bf16[160,1280]{1,0:T(8,128)(2,1)S(1)} %collective-permute-done.11.refs_2_, ...), custom_call_target="tpu_custom_call" | custom-call | tf_op jit(solution)/shard_map/assemble/pallas_call | solution.py:303
  68.7 0.0 collective-permute-done.7.refs_0_
  68.7 3.1 %collective-permute-done.8.refs_1_ = bf16[88,1024]{1,0:T(8,128)(2,1)S(1)} collective-permute-done((bf16[88,1024]{1,0:T(8,128)(2,1)}, bf16[88,1024]{1,0:T(8,128)(2,1)S(1)}, u32[]{:S(2)}, u32[]{:S(2)}) %collective-permute-start.8) | collective-permute-done | bytes 180256 | tf_op jit(solution)/shard_map/ppermute | solution.py:432
  71.9 4.6 %collective-permute-done.9.refs_2_ = bf16[88,1024]{1,0:T(8,128)(2,1)} collective-permute-done((bf16[88,1024]{1,0:T(8,128)(2,1)}, bf16[88,1024]{1,0:T(8,128)(2,1)}, u32[]{:S(2)}, u32[]{:S(2)}) %collective-permute-start.9) | collective-permute-done | bytes 180256 | tf_op jit(solution)/shard_map/ppermute | solution.py:432
  76.4 0.4 collective-permute-start.17
  76.8 1.1 combine.1.refs_0_
  78.0 0.2 collective-permute-start.13
  78.2 2.0 %collective-permute-done.13.refs_1_ = bf16[80,1024]{1,0:T(8,128)(2,1)S(1)} collective-permute-done((bf16[80,1024]{1,0:T(8,128)(2,1)S(1)}, bf16[80,1024]{1,0:T(8,128)(2,1)S(1)}, u32[]{:S(2)}, u32[]{:S(2)}) %collective-permute-start.13) | collective-permute-done | bytes 163872 | tf_op jit(solution)/shard_map/ppermute | solution.py:441
  80.2 0.0 copy-start.1
  80.2 0.0 copy-start.2
  80.3 0.0 copy-start.3
  80.3 0.0 copy-start
  80.3 0.9 collective-permute-start.14
  81.2 1.8 %collective-permute-start.15 = (bf16[160,1024]{1,0:T(8,128)(2,1)S(1)}, bf16[160,1024]{1,0:T(8,128)(2,1)S(1)}, u32[]{:S(2)}, u32[]{:S(2)}) collective-permute-start(bf16[160,1024]{1,0:T(8,128)(2,1)S(1)} %pad_maximum_fusion.1), channel_id=1, source_target_pairs={{0,8},{1,9},{2,3},{3,2},{4,12},{5,13},{6,7},{7,6},{8,0},{9,1},{10,... | collective-permute-start | bytes 983048 | tf_op jit(solution)/shard_map/ppermute | solution.py:441
  83.0 2.0 %collective-permute-start.16 = (bf16[160,1024]{1,0:T(8,128)(2,1)S(1)}, bf16[160,1024]{1,0:T(8,128)(2,1)S(1)}, u32[]{:S(2)}, u32[]{:S(2)}) collective-permute-start(bf16[160,1024]{1,0:T(8,128)(2,1)S(1)} %pad_maximum_fusion.1), channel_id=1, source_target_pairs={{0,5},{1,4},{2,15},{3,14},{4,9},{5,8},{6,3},{7,2},{8,13},{9,12},{1... | collective-permute-start | bytes 983048 | tf_op jit(solution)/shard_map/ppermute | solution.py:441
  85.0 2.8 %collective-permute-start.18 = (bf16[80,1024]{1,0:T(8,128)(2,1)S(1)}, bf16[80,1024]{1,0:T(8,128)(2,1)S(1)}, u32[]{:S(2)}, u32[]{:S(2)}) collective-permute-start(bf16[80,1024]{1,0:T(8,128)(2,1)S(1)} %combine.1.refs_0_), channel_id=1, source_target_pairs={{0,9},{1,8},{2,11},{3,10},{4,13},{5,12},{6,15},{7,14},{8,1},{9,0},... | collective-permute-start | bytes 491528 | tf_op jit(solution)/shard_map/ppermute | solution.py:441
  87.9 0.0 collective-permute-done.14.refs_2_
  87.9 6.2 %collective-permute-start.19 = (bf16[160,1024]{1,0:T(8,128)(2,1)S(1)}, bf16[160,1024]{1,0:T(8,128)(2,1)S(1)}, u32[]{:S(2)}, u32[]{:S(2)}) collective-permute-start(bf16[160,1024]{1,0:T(8,128)(2,1)S(1)} %collective-permute-done.14.refs_2_), channel_id=1, source_target_pairs={{0,2},{1,3},{2,0},{3,1},{4,6},{5,7},{6,4},{7,5},{8,10},{9,11},{10,... | collective-permute-start | bytes 983048 | tf_op jit(solution)/shard_map/ppermute | solution.py:441
  94.1 0.0 collective-permute-done.15.refs_3_
  94.1 0.0 collective-permute-start.20
  94.1 1.6 %collective-permute-done.16.refs_4_ = bf16[160,1024]{1,0:T(8,128)(2,1)S(1)} collective-permute-done((bf16[160,1024]{1,0:T(8,128)(2,1)S(1)}, bf16[160,1024]{1,0:T(8,128)(2,1)S(1)}, u32[]{:S(2)}, u32[]{:S(2)}) %collective-permute-start.16) | collective-permute-done | bytes 327712 | tf_op jit(solution)/shard_map/ppermute | solution.py:441
  95.7 3.8 %collective-permute-start.21 = (bf16[160,1024]{1,0:T(8,128)(2,1)S(1)}, bf16[160,1024]{1,0:T(8,128)(2,1)S(1)}, u32[]{:S(2)}, u32[]{:S(2)}) collective-permute-start(bf16[160,1024]{1,0:T(8,128)(2,1)S(1)} %collective-permute-done.16.refs_4_), channel_id=1, source_target_pairs={{0,2},{1,3},{2,0},{3,1},{4,6},{5,7},{6,4},{7,5},{8,10},{9,11},{10,... | collective-permute-start | bytes 983048 | tf_op jit(solution)/shard_map/ppermute | solution.py:441
  99.5 0.0 collective-permute-done.17.refs_1_
  99.5 0.4 join.1.refs_10_
  99.9 0.0 collective-permute-done.18.refs_5_
  99.9 2.2 %collective-permute-start.22 = (bf16[80,1024]{1,0:T(8,128)(2,1)S(1)}, bf16[80,1024]{1,0:T(8,128)(2,1)S(1)}, u32[]{:S(2)}, u32[]{:S(2)}) collective-permute-start(bf16[80,1024]{1,0:T(8,128)(2,1)S(1)} %collective-permute-done.18.refs_5_), channel_id=1, source_target_pairs={{0,2},{1,3},{2,0},{3,1},{4,6},{5,7},{6,4},{7,5},{8,10},{9,11},{10,... | collective-permute-start | bytes 491528 | tf_op jit(solution)/shard_map/ppermute | solution.py:441
  102.1 0.0 copy-done.1
  102.1 0.0 copy-done.2
  102.2 0.0 copy-done.3
  102.2 0.0 collective-permute-done.19.refs_6_
  102.2 0.0 collective-permute-done.20.refs_7_
  102.2 0.0 collective-permute-done.21.refs_8_
  102.2 0.9 collective-permute-done.22.refs_9_
  103.2 0.0 copy-done
  103.2 12.7 %project.1 = bf16[320,256]{1,0:T(8,128)(2,1)} custom-call(s32[24]{0:T(128)S(1)} %dynamic-slice_bitcast_fusion.heads, bf16[80,1024]{1,0:T(8,128)(2,1)S(1)} %combine.1.refs_0_, bf16[80,1024]{1,0:T(8,128)(2,1)S(1)} %collective-permute-done.13.refs_1_, bf16[160,1024]{1,0:T(8,128)(2,1)S(1)} %collective-permute-done.14.refs_2_, ...), custom_call_target="tpu_custom_call" | custom-call | tf_op jit(solution)/shard_map/project/pallas_call | solution.py:377
  (4 shorter events, 0.0 us)
Async XLA Ops:
  0.0 24.4 %collective-permute-start = (bf16[80,1280]{1,0:T(8,128)(2,1)}, bf16[80,1280]{1,0:T(8,128)(2,1)S(1)}, u32[]{:S(2)}, u32[]{:S(2)}) collective-permute-start(bf16[80,1280]{1,0:T(8,128)(2,1)} %param.14), channel_id=1, source_target_pairs={{0,1},{1,0},{2,3},{3,2},{4,5},{5,4},{6,7},{7,6},{8,9},{9,8},{10,11... | collective-permute-start | bytes 614408 | tf_op jit(solution)/shard_map/ppermute | solution.py:441
  4.9 11.0 %collective-permute-start.1 = (bf16[88,1024]{1,0:T(8,128)(2,1)S(1)}, bf16[88,1024]{1,0:T(8,128)(2,1)S(1)}, u32[]{:S(2)}, u32[]{:S(2)}) collective-permute-start(bf16[88,1024]{1,0:T(8,128)(2,1)S(1)} %get-tuple-element.49.refs_0_.query), channel_id=1, source_target_pairs={{0,64},{2,66},{4,68},{6,70},{8,72},{10,74},{12,76},{14,78},{16,80}... | collective-permute-start | bytes 540680 | tf_op jit(solution)/shard_map/ppermute | solution.py:432
  11.9 25.4 %collective-permute-start.4 = (bf16[168,1024]{1,0:T(8,128)(2,1)S(1)}, bf16[168,1024]{1,0:T(8,128)(2,1)S(1)}, u32[]{:S(2)}, u32[]{:S(2)}) collective-permute-start(bf16[168,1024]{1,0:T(8,128)(2,1)S(1)} %get-tuple-element.41.refs_4_), channel_id=1, source_target_pairs={{0,16},{2,114},{4,20},{6,118},{8,24},{10,122},{12,28},{14,126},{16... | collective-permute-start | bytes 1032200 | tf_op jit(solution)/shard_map/ppermute | solution.py:432
  11.9 25.4 %collective-permute-start.5 = (bf16[168,1024]{1,0:T(8,128)(2,1)S(1)}, bf16[168,1024]{1,0:T(8,128)(2,1)S(1)}, u32[]{:S(2)}, u32[]{:S(2)}) collective-permute-start(bf16[168,1024]{1,0:T(8,128)(2,1)S(1)} %get-tuple-element.41.refs_4_), channel_id=1, source_target_pairs={{0,128},{2,130},{4,132},{6,134},{8,136},{10,138},{12,140},{14,142}... | collective-permute-start | bytes 1032200 | tf_op jit(solution)/shard_map/ppermute | solution.py:432
  12.3 25.0 %collective-permute-start.6 = (bf16[168,1024]{1,0:T(8,128)(2,1)S(1)}, bf16[168,1024]{1,0:T(8,128)(2,1)S(1)}, u32[]{:S(2)}, u32[]{:S(2)}) collective-permute-start(bf16[168,1024]{1,0:T(8,128)(2,1)S(1)} %get-tuple-element.41.refs_4_), channel_id=1, source_target_pairs={{0,144},{2,242},{4,148},{6,246},{8,152},{10,250},{12,156},{14,254}... | collective-permute-start | bytes 1032200 | tf_op jit(solution)/shard_map/ppermute | solution.py:432
  15.9 16.8 %collective-permute-start.2 = (bf16[88,1024]{1,0:T(8,128)(2,1)S(1)}, bf16[88,1024]{1,0:T(8,128)(2,1)S(1)}, u32[]{:S(2)}, u32[]{:S(2)}) collective-permute-start(bf16[88,1024]{1,0:T(8,128)(2,1)S(1)} %get-tuple-element.49.refs_0_.query), channel_id=1, source_target_pairs={{0,160},{2,226},{4,164},{6,230},{8,168},{10,234},{12,172},{14,238}... | collective-permute-start | bytes 540680 | tf_op jit(solution)/shard_map/ppermute | solution.py:432
  24.4 12.8 %collective-permute-start.3 = (bf16[88,1024]{1,0:T(8,128)(2,1)S(1)}, bf16[88,1024]{1,0:T(8,128)(2,1)S(1)}, u32[]{:S(2)}, u32[]{:S(2)}) collective-permute-start(bf16[88,1024]{1,0:T(8,128)(2,1)S(1)} %get-tuple-element.49.refs_0_.query), channel_id=1, source_target_pairs={{0,224},{2,162},{4,228},{6,166},{8,232},{10,170},{12,236},{14,174}... | collective-permute-start | bytes 540680 | tf_op jit(solution)/shard_map/ppermute | solution.py:432
  37.3 22.2 %collective-permute-start.10 = (bf16[160,1280]{1,0:T(8,128)(2,1)S(1)}, bf16[160,1280]{1,0:T(8,128)(2,1)S(1)}, u32[]{:S(2)}, u32[]{:S(2)}) collective-permute-start(bf16[160,1280]{1,0:T(8,128)(2,1)S(1)} %pad_maximum_fusion.refs_0_), channel_id=1, source_target_pairs={{0,4},{1,5},{2,6},{3,7},{4,8},{5,9},{6,10},{7,11},{8,12},{9,13},{1... | collective-permute-start | bytes 1228808 | tf_op jit(solution)/shard_map/ppermute | solution.py:441
  38.6 26.9 %collective-permute-start.11 = (bf16[160,1280]{1,0:T(8,128)(2,1)S(1)}, bf16[160,1280]{1,0:T(8,128)(2,1)S(1)}, u32[]{:S(2)}, u32[]{:S(2)}) collective-permute-start(bf16[160,1280]{1,0:T(8,128)(2,1)S(1)} %pad_maximum_fusion.refs_0_), channel_id=1, source_target_pairs={{0,12},{1,13},{2,14},{3,15},{4,0},{5,1},{6,2},{7,3},{8,4},{9,5},{1... | collective-permute-start | bytes 1228808 | tf_op jit(solution)/shard_map/ppermute | solution.py:441
  40.0 25.4 %collective-permute-start.12 = (bf16[160,1280]{1,0:T(8,128)(2,1)S(1)}, bf16[160,1280]{1,0:T(8,128)(2,1)}, u32[]{:S(2)}, u32[]{:S(2)}) collective-permute-start(bf16[160,1280]{1,0:T(8,128)(2,1)S(1)} %pad_maximum_fusion.refs_0_), channel_id=1, source_target_pairs={{0,8},{1,9},{2,10},{3,11},{4,12},{5,13},{6,14},{7,15},{8,0},{9,1},... | collective-permute-start | bytes 1228808 | tf_op jit(solution)/shard_map/ppermute | solution.py:441
  51.2 17.5 %collective-permute-start.7 = (bf16[88,1024]{1,0:T(8,128)(2,1)}, bf16[88,1024]{1,0:T(8,128)(2,1)S(1)}, u32[]{:S(2)}, u32[]{:S(2)}) collective-permute-start(bf16[88,1024]{1,0:T(8,128)(2,1)} %get-tuple-element.45), channel_id=1, source_target_pairs={{0,64},{2,66},{4,68},{6,70},{8,72},{10,74},{12,76},{14,78},{16,80}... | collective-permute-start | bytes 540680 | tf_op jit(solution)/shard_map/ppermute | solution.py:432
  55.6 16.3 %collective-permute-start.8 = (bf16[88,1024]{1,0:T(8,128)(2,1)}, bf16[88,1024]{1,0:T(8,128)(2,1)S(1)}, u32[]{:S(2)}, u32[]{:S(2)}) collective-permute-start(bf16[88,1024]{1,0:T(8,128)(2,1)} %get-tuple-element.46), channel_id=1, source_target_pairs={{0,160},{2,226},{4,164},{6,230},{8,168},{10,234},{12,172},{14,238}... | collective-permute-start | bytes 540680 | tf_op jit(solution)/shard_map/ppermute | solution.py:432
  59.5 17.0 %collective-permute-start.9 = (bf16[88,1024]{1,0:T(8,128)(2,1)}, bf16[88,1024]{1,0:T(8,128)(2,1)}, u32[]{:S(2)}, u32[]{:S(2)}) collective-permute-start(bf16[88,1024]{1,0:T(8,128)(2,1)} %get-tuple-element.47), channel_id=1, source_target_pairs={{0,224},{2,162},{4,228},{6,166},{8,232},{10,170},{12,236},{14,174}... | collective-permute-start | bytes 540680 | tf_op jit(solution)/shard_map/ppermute | solution.py:432
  76.4 23.0 %collective-permute-start.17 = (bf16[640,1280]{1,0:T(8,128)(2,1)S(1)}, bf16[640,1280]{1,0:T(8,128)(2,1)S(1)}, u32[]{:S(2)}, u32[]{:S(2)}) collective-permute-start(bf16[640,1280]{1,0:T(8,128)(2,1)S(1)} %assemble.1.refs_0_), channel_id=1, source_target_pairs={{0,2},{1,3},{2,0},{3,1},{4,6},{5,7},{6,4},{7,5},{8,10},{9,11},{10,... | collective-permute-start | bytes 4915208 | tf_op jit(solution)/shard_map/ppermute | solution.py:441
  78.0 2.2 %collective-permute-start.13 = (bf16[80,1024]{1,0:T(8,128)(2,1)S(1)}, bf16[80,1024]{1,0:T(8,128)(2,1)S(1)}, u32[]{:S(2)}, u32[]{:S(2)}) collective-permute-start(bf16[80,1024]{1,0:T(8,128)(2,1)S(1)} %combine.1.refs_0_), channel_id=1, source_target_pairs={{0,2},{1,3},{2,0},{3,1},{4,6},{5,7},{6,4},{7,5},{8,10},{9,11},{10,... | collective-permute-start | bytes 491528 | tf_op jit(solution)/shard_map/ppermute | solution.py:441
  80.2 21.9 %copy-start.1 = (f32[1280]{0:T(1024)S(1)}, f32[1280]{0:T(1024)}, u32[]{:S(2)}) copy-start(f32[1280]{0:T(1024)} %param.15) | copy-start | bytes 15364
  80.2 21.9 %copy-start.2 = (f32[1280]{0:T(1024)S(1)}, f32[1280]{0:T(1024)}, u32[]{:S(2)}) copy-start(f32[1280]{0:T(1024)} %param.16) | copy-start | bytes 15364
  80.3 21.9 %copy-start.3 = (f32[320]{0:T(512)S(1)}, f32[320]{0:T(512)}, u32[]{:S(2)}) copy-start(f32[320]{0:T(512)} %param.18) | copy-start | bytes 3844
  80.3 22.9 %copy-start = (bf16[5120,320]{0,1:T(8,128)(2,1)S(1)}, bf16[5120,320]{0,1:T(8,128)(2,1)}, u32[]{:S(2)}) copy-start(bf16[5120,320]{0,1:T(8,128)(2,1)} %param.17) | copy-start | bytes 9830404
  80.3 7.6 %collective-permute-start.14 = (bf16[160,1024]{1,0:T(8,128)(2,1)S(1)}, bf16[160,1024]{1,0:T(8,128)(2,1)S(1)}, u32[]{:S(2)}, u32[]{:S(2)}) collective-permute-start(bf16[160,1024]{1,0:T(8,128)(2,1)S(1)} %pad_maximum_fusion.1), channel_id=1, source_target_pairs={{0,4},{1,5},{2,14},{3,15},{4,8},{5,9},{6,2},{7,3},{8,12},{9,13},{1... | collective-permute-start | bytes 983048 | tf_op jit(solution)/shard_map/ppermute | solution.py:441
  81.2 12.9 %collective-permute-start.15 = (bf16[160,1024]{1,0:T(8,128)(2,1)S(1)}, bf16[160,1024]{1,0:T(8,128)(2,1)S(1)}, u32[]{:S(2)}, u32[]{:S(2)}) collective-permute-start(bf16[160,1024]{1,0:T(8,128)(2,1)S(1)} %pad_maximum_fusion.1), channel_id=1, source_target_pairs={{0,8},{1,9},{2,3},{3,2},{4,12},{5,13},{6,7},{7,6},{8,0},{9,1},{10,... | collective-permute-start | bytes 983048 | tf_op jit(solution)/shard_map/ppermute | solution.py:441
  83.0 12.7 %collective-permute-start.16 = (bf16[160,1024]{1,0:T(8,128)(2,1)S(1)}, bf16[160,1024]{1,0:T(8,128)(2,1)S(1)}, u32[]{:S(2)}, u32[]{:S(2)}) collective-permute-start(bf16[160,1024]{1,0:T(8,128)(2,1)S(1)} %pad_maximum_fusion.1), channel_id=1, source_target_pairs={{0,5},{1,4},{2,15},{3,14},{4,9},{5,8},{6,3},{7,2},{8,13},{9,12},{1... | collective-permute-start | bytes 983048 | tf_op jit(solution)/shard_map/ppermute | solution.py:441
  85.0 14.9 %collective-permute-start.18 = (bf16[80,1024]{1,0:T(8,128)(2,1)S(1)}, bf16[80,1024]{1,0:T(8,128)(2,1)S(1)}, u32[]{:S(2)}, u32[]{:S(2)}) collective-permute-start(bf16[80,1024]{1,0:T(8,128)(2,1)S(1)} %combine.1.refs_0_), channel_id=1, source_target_pairs={{0,9},{1,8},{2,11},{3,10},{4,13},{5,12},{6,15},{7,14},{8,1},{9,0},... | collective-permute-start | bytes 491528 | tf_op jit(solution)/shard_map/ppermute | solution.py:441
  87.9 14.3 %collective-permute-start.19 = (bf16[160,1024]{1,0:T(8,128)(2,1)S(1)}, bf16[160,1024]{1,0:T(8,128)(2,1)S(1)}, u32[]{:S(2)}, u32[]{:S(2)}) collective-permute-start(bf16[160,1024]{1,0:T(8,128)(2,1)S(1)} %collective-permute-done.14.refs_2_), channel_id=1, source_target_pairs={{0,2},{1,3},{2,0},{3,1},{4,6},{5,7},{6,4},{7,5},{8,10},{9,11},{10,... | collective-permute-start | bytes 983048 | tf_op jit(solution)/shard_map/ppermute | solution.py:441
  94.1 8.1 %collective-permute-start.20 = (bf16[160,1024]{1,0:T(8,128)(2,1)S(1)}, bf16[160,1024]{1,0:T(8,128)(2,1)S(1)}, u32[]{:S(2)}, u32[]{:S(2)}) collective-permute-start(bf16[160,1024]{1,0:T(8,128)(2,1)S(1)} %collective-permute-done.15.refs_3_), channel_id=1, source_target_pairs={{0,2},{1,3},{2,0},{3,1},{4,6},{5,7},{6,4},{7,5},{8,10},{9,11},{10,... | collective-permute-start | bytes 983048 | tf_op jit(solution)/shard_map/ppermute | solution.py:441
  95.7 6.5 %collective-permute-start.21 = (bf16[160,1024]{1,0:T(8,128)(2,1)S(1)}, bf16[160,1024]{1,0:T(8,128)(2,1)S(1)}, u32[]{:S(2)}, u32[]{:S(2)}) collective-permute-start(bf16[160,1024]{1,0:T(8,128)(2,1)S(1)} %collective-permute-done.16.refs_4_), channel_id=1, source_target_pairs={{0,2},{1,3},{2,0},{3,1},{4,6},{5,7},{6,4},{7,5},{8,10},{9,11},{10,... | collective-permute-start | bytes 983048 | tf_op jit(solution)/shard_map/ppermute | solution.py:441
  99.9 3.3 %collective-permute-start.22 = (bf16[80,1024]{1,0:T(8,128)(2,1)S(1)}, bf16[80,1024]{1,0:T(8,128)(2,1)S(1)}, u32[]{:S(2)}, u32[]{:S(2)}) collective-permute-start(bf16[80,1024]{1,0:T(8,128)(2,1)S(1)} %collective-permute-done.18.refs_5_), channel_id=1, source_target_pairs={{0,2},{1,3},{2,0},{3,1},{4,6},{5,7},{6,4},{7,5},{8,10},{9,11},{10,... | collective-permute-start | bytes 491528 | tf_op jit(solution)/shard_map/ppermute | solution.py:441
where the time goes:
time: 117 us; the launch traced here: 116 us
  starting transfers between devices  56.1 us (48%)
  Pallas kernels  33.5 us (29%)
  waiting for transfers between devices  24.4 us (21%)
    ppermute x14, starting transfers between devices, send(): return lax.ppermute(block, GROUP, perm)  28.4 us
    ppermute x9, starting transfers between devices, swap(): return lax.ppermute(block, ('blk', 'section'), perm)  27.7 us
    ppermute x9, waiting for transfers between devices, swap(): return lax.ppermute(block, ('blk', 'section'), perm)  19.7 us
    pallas_call x1, Pallas kernels, project(): pl.pallas_call(functools.partial(project_kernel, count), out_shape=jax.Sh...  12.7 us
    pallas_call x1, Pallas kernels, attend_first(): pl.pallas_call(functools.partial(attend_first_kernel, blocks), out_shape=...  9.6 us
    pallas_call x1, Pallas kernels, attend_next(): pl.pallas_call(functools.partial(attend_next_kernel, block), out_shape=ja...  5.27 us
    ppermute x14, waiting for transfers between devices, send(): return lax.ppermute(block, GROUP, perm)  4.63 us
    pallas_call x1, Pallas kernels, assemble(): pl.pallas_call(assemble_kernel, out_shape=jax.ShapeDtypeStruct((8 * HDIM,...  3.26 us
  transfers between devices with their start and end apart: 23, of which 8 were waited for; matrix products, arithmetic and copies ran while one was open for 1% of the time, Pallas kernels for 18%

commit v1 on v0

--- a/solution.py
+++ b/solution.py
@@ -106,18 +106,24 @@
 
         def key_block_step(kb, started):
             low, high = limits[4 + kb, 0], limits[4 + kb, 3]
-            whole = jnp.logical_and(jnp.logical_and(low == high, q_low == q_high), low == q_low)
-            still = jnp.logical_and(jnp.logical_and(whole, started > 0), keep_shift)
+            live = jnp.logical_and(low <= q_high, high >= q_low)
+            pure = q_low == q_high
+            still = jnp.logical_and(
+                jnp.logical_and(pure, jnp.logical_and(low == high, low == q_low)), keep_shift
+            )
+
+            @pl.when(jnp.logical_and(still, started == 0))
+            def _():
+                for j in range(count // sub):
+                    columns = slice(j * sub, (j + 1) * sub)
+                    found = jnp.dot(held_k[kb, 0:128, :], query[0:80, columns], preferred_element_type=f32)
+                    row_max[:, columns] = jnp.max(found, axis=0, keepdims=True)
 
             @pl.when(still)
             def _():
                 tile(kb, 0, count, False, False)
 
-            @pl.when(jnp.logical_and(whole, jnp.logical_not(still)))
-            def _():
-                tile(kb, 0, count, False, True)
-
-            @pl.when(jnp.logical_not(whole))
+            @pl.when(jnp.logical_and(live, jnp.logical_not(still)))
             def _():
                 def half(t, unused):
                     low, high = limits[4 + kb, 2 * t], limits[4 + kb, 2 * t + 1]
@@ -130,7 +136,7 @@
 
                 lax.fori_loop(0, tiles, half, 0)
 
-            return jnp.maximum(started, whole.astype(jnp.int32))
+            return jnp.maximum(started, live.astype(jnp.int32))
 
         lax.fori_loop(0, 4, key_block_step, 0)
 
@@ -159,22 +165,8 @@
     out[80:88, :] = jnp.concatenate(rows, axis=0).astype(bf16)
 
 
-def copy_limits(limits, limits_s, sem):
-    copy = pltpu.make_async_copy(limits, limits_s, sem)
-    copy.start()
-    copy.wait()
-
-
-def attend_first_kernel(blocks, *refs):
-    queries, key_values = refs[0:4], refs[4:8]
-    outs = refs[8 : 8 + len(blocks)]
-    (held_k, held_v, limits, query, ids, limits_s, row_max, total, excess, sem) = refs[8 + len(blocks) :]
-    count = queries[0].shape[1]
-    for i in range(4):
-        held_k[i] = key_values[i][0:80, :].T
-        held_v[i] = key_values[i][80:168, :]
-        ids[i : i + 1, :] = queries[i][80:88, :].astype(f32)[0:1, :]
-        ids[4 + i : 5 + i, :] = key_values[i][160:168, :].astype(f32)[1:2, :]
+def find_limits(ids, limits, limits_s, sem):
+    count = ids.shape[1]
     lane = lax.broadcasted_iota(jnp.int32, (8, 128), 1)
     table = jnp.zeros((8, 128), f32)
     for t in range(2):
@@ -182,13 +174,35 @@
         table = jnp.where(lane == 2 * t, jnp.min(part, axis=1, keepdims=True), table)
         table = jnp.where(lane == 2 * t + 1, jnp.max(part, axis=1, keepdims=True), table)
     limits[...] = table.astype(jnp.int32)
-    copy_limits(limits, limits_s, sem)
-    for i, block in enumerate(blocks):
-        query[i] = queries[block][...]
+    copy = pltpu.make_async_copy(limits, limits_s, sem)
+    copy.start()
+    copy.wait()
+
+
+def attend_kernel(blocks, first, *refs):
+    queries, refs = refs[:blocks], refs[blocks:]
+    if first:
+        key_values, refs = refs[:4], refs[4:]
+    else:
+        (held_k, held_v), refs = refs[:2], refs[2:]
+    outs, refs = refs[:blocks], refs[blocks:]
+    if first:
+        (held_k, held_v), refs = refs[:2], refs[2:]
+    query, ids, limits, limits_s, row_max, total, excess, sem = refs
+    ids[...] = jnp.zeros_like(ids)
+    for i in range(4):
+        if first:
+            held_k[i] = key_values[i][0:80, :].T
+            held_v[i] = key_values[i][80:168, :]
+        ids[4 + i : 5 + i, :] = held_v[i, 80:88, :].astype(f32)[1:2, :]
+    for i in range(blocks):
+        query[i] = queries[i][...]
+        ids[i : i + 1, :] = queries[i][80:88, :].astype(f32)[0:1, :]
+    find_limits(ids, limits, limits_s, sem)
 
     def one(i, unused):
-        attend_block(query.at[i], held_k, held_v, limits_s, blocks[0] + i, row_max, total, excess)
-        for o in range(len(blocks)):
+        attend_block(query.at[i], held_k, held_v, limits_s, i, row_max, total, excess)
+        for o in range(blocks):
 
             @pl.when(i == o)
             def _():
@@ -196,24 +210,26 @@
 
         return 0
 
-    lax.fori_loop(0, len(blocks), one, 0)
-
-
-def attend_first(queries, key_values, blocks):
+    lax.fori_loop(0, blocks, one, 0)
+
+
+def attend(queries, key_values, held=None):
     count = queries[0].shape[1]
-    return pl.pallas_call(
-        functools.partial(attend_first_kernel, blocks),
-        out_shape=[jax.ShapeDtypeStruct((88, count), bf16)] * len(blocks)
-        + [
-            jax.ShapeDtypeStruct((4, count, 80), bf16),
-            jax.ShapeDtypeStruct((4, 88, count), bf16),
-            jax.ShapeDtypeStruct((8, 128), jnp.int32),
-        ],
-        in_specs=[IN_VMEM] * 8,
-        out_specs=[IN_VMEM] * (3 + len(blocks)),
+    first = held is None
+    shapes = [jax.ShapeDtypeStruct((88, count), bf16)] * len(queries)
+    if first:
+        shapes.append(jax.ShapeDtypeStruct((4, count, 80), bf16))
+        shapes.append(jax.ShapeDtypeStruct((4, 88, count), bf16))
+    operands = list(queries) + list(key_values if first else held)
+    out = pl.pallas_call(
+        functools.partial(attend_kernel, len(queries), first),
+        out_shape=shapes,
+        in_specs=[IN_VMEM] * len(operands),
+        out_specs=[IN_VMEM] * len(shapes),
         scratch_shapes=[
-            pltpu.VMEM((len(blocks), 88, count), bf16),
+            pltpu.VMEM((len(queries), 88, count), bf16),
             pltpu.VMEM((8, count), f32),
+            pltpu.VMEM((8, 128), jnp.int32),
             pltpu.SMEM((8, 128), jnp.int32),
             pltpu.VMEM((1, count), f32),
             pltpu.VMEM((88, count), f32),
@@ -221,35 +237,9 @@
             pltpu.SemaphoreType.DMA,
         ],
         compiler_params=pltpu.CompilerParams(vmem_limit_bytes=16 << 20),
-        name="attend_first",
-    )(*queries, *key_values)
-
-
-def attend_next_kernel(
-    block, query, held_k, held_v, limits, out, limits_s, row_max, total, excess, sem
-):
-    copy_limits(limits, limits_s, sem)
-    attend_block(query, held_k, held_v, limits_s, block, row_max, total, excess)
-    store_partial(out, row_max, total)
-
-
-def attend_next(block, query, held_k, held_v, limits):
-    count = query.shape[1]
-    return pl.pallas_call(
-        functools.partial(attend_next_kernel, block),
-        out_shape=jax.ShapeDtypeStruct((88, count), bf16),
-        in_specs=[IN_VMEM] * 4,
-        out_specs=IN_VMEM,
-        scratch_shapes=[
-            pltpu.SMEM((8, 128), jnp.int32),
-            pltpu.VMEM((1, count), f32),
-            pltpu.VMEM((88, count), f32),
-            pltpu.VMEM((1, count), f32),
-            pltpu.SemaphoreType.DMA,
-        ],
-        compiler_params=pltpu.CompilerParams(vmem_limit_bytes=12 << 20),
-        name="attend_next",
-    )(query, held_k, held_v, limits)
+        name="attend_first" if first else "attend_next",
+    )(*operands)
+    return list(out[: len(queries)]), list(out[len(queries) :])
 
 
 def combine_kernel(*refs):
@@ -440,7 +430,6 @@
                     perm.append(((x * 2 + c) * 2 + t, (a % 4 * 2 + b) * 2 + d))
         return lax.ppermute(block, GROUP, perm)
 
-    far = send(out_weight, lambda x, c, t: (x, c, 1 - t))
     me = lax.axis_index("section") * 2 + lax.axis_index("tp")
     heads = jnp.asarray(head_order(), jnp.int32)[me]
 
@@ -448,15 +437,20 @@
         return x, 1 - c, t
 
     key_blocks = [swap(key_block, mask) for mask in KEY_PARTNERS]
-    query_blocks = [swap(query_block, mask) for mask in QUERY_PARTNERS]
-    both = jnp.concatenate([out_weight, far], axis=0)
-    both, query_blocks, key_blocks = lax.optimization_barrier((both, query_blocks, key_blocks))
+    queries_at = [query_block, swap(query_block, QUERY_PARTNERS[1])]
+    late_query, late_weight, _ = lax.optimization_barrier(
+        (query_block, out_weight, (key_blocks, queries_at[1]))
+    )
+    queries_at += [swap(late_query, mask) for mask in QUERY_PARTNERS[2:]]
+    far = send(late_weight, lambda x, c, t: (x, c, 1 - t))
+    returned, held = attend(queries_at[:2], key_blocks)
+    both = jnp.concatenate([late_weight, far], axis=0)
+    returned[1] = swap(returned[1], QUERY_PARTNERS[1])
+    both, late_queries, held = lax.optimization_barrier((both, queries_at[2:], held))
     weights = [both] + [send(both, lambda x, c, t, d=d: (x + d, c, t)) for d in (1, 3, 2)]
-    *partial, held_k, held_v, limits = attend_first(query_blocks, key_blocks, (1, 2, 3))
-    returned = [swap(part, mask) for part, mask in zip(partial, QUERY_PARTNERS[1:])]
-    own_query, partial = lax.optimization_barrier((query_blocks[0], partial))
-    returned.append(attend_next(0, own_query, held_k, held_v, limits))
-    weights, returned[3] = lax.optimization_barrier((weights, returned[3]))
+    late, _ = attend(late_queries, None, held)
+    returned += [swap(part, mask) for part, mask in zip(late, QUERY_PARTNERS[2:])]
+    weights, late = lax.optimization_barrier((weights, late))
     half = assemble(heads, weights)
     returned, half = lax.optimization_barrier((returned, half))
     other_half = send(half, across)

time: 117 us -> 114 us (0.974)
  the two profiles are of different devices: /device:TPU:1 before, /device:TPU:71 now
where the time goes in v1:
time: 114 us; the launch traced here: 113 us
  starting transfers between devices  63.5 us (56%)
  Pallas kernels  29.7 us (26%)
  waiting for transfers between devices  18.1 us (16%)
    ppermute x14, starting transfers between devices, send(): return lax.ppermute(block, GROUP, perm)  34.8 us
    ppermute x9, starting transfers between devices, swap(): return lax.ppermute(block, ('blk', 'section'), perm)  28.7 us
    pallas_call x1, Pallas kernels, project(): pl.pallas_call(functools.partial(project_kernel, count), out_shape=jax.Sh...  12.7 us
    pallas_call x2, Pallas kernels, attend(): pl.pallas_call(functools.partial(attend_kernel, len(queries), first), out...  12.5 us
    ppermute x9, waiting for transfers between devices, swap(): return lax.ppermute(block, ('blk', 'section'), perm)  11.8 us
    ppermute x14, waiting for transfers between devices, send(): return lax.ppermute(block, GROUP, perm)  6.24 us
    pallas_call x1, Pallas kernels, assemble(): pl.pallas_call(assemble_kernel, out_shape=jax.ShapeDtypeStruct((8 * HDIM,...  2.78 us
  transfers between devices with their start and end apart: 23, of which 9 were waited for; matrix products, arithmetic and copies ran while one was open for 1% of the time, Pallas kernels for 14%

profile of v1, /device:TPU:71, one launch (start us, length us, event | category | flops | bytes accessed | tf_op | source)
XLA Modules:
  0.0 113.4 jit_solution(14295454721148591751)
XLA Ops:
  0.0 1.1 pack.1
  1.1 0.1 collective-permute-start.1
  1.2 1.4 %collective-permute-start.2 = (bf16[168,1024]{1,0:T(8,128)(2,1)S(1)}, bf16[168,1024]{1,0:T(8,128)(2,1)S(1)}, u32[]{:S(2)}, u32[]{:S(2)}) collective-permute-start(bf16[168,1024]{1,0:T(8,128)(2,1)S(1)} %get-tuple-element.32.refs_2_), channel_id=1, source_target_pairs={{0,128},{2,130},{4,132},{6,134},{8,136},{10,138},{12,140},{14,142}... | collective-permute-start | bytes 1032200 | tf_op jit(solution)/shard_map/ppermute | solution.py:422
  2.6 1.3 %collective-permute-start.3 = (bf16[168,1024]{1,0:T(8,128)(2,1)S(1)}, bf16[168,1024]{1,0:T(8,128)(2,1)S(1)}, u32[]{:S(2)}, u32[]{:S(2)}) collective-permute-start(bf16[168,1024]{1,0:T(8,128)(2,1)S(1)} %get-tuple-element.32.refs_2_), channel_id=1, source_target_pairs={{0,144},{2,242},{4,148},{6,246},{8,152},{10,250},{12,156},{14,254}... | collective-permute-start | bytes 1032200 | tf_op jit(solution)/shard_map/ppermute | solution.py:422
  3.9 5.1 %collective-permute-start = (bf16[88,1024]{1,0:T(8,128)(2,1)S(1)}, bf16[88,1024]{1,0:T(8,128)(2,1)S(1)}, u32[]{:S(2)}, u32[]{:S(2)}) collective-permute-start(bf16[88,1024]{1,0:T(8,128)(2,1)S(1)} %get-tuple-element.36.refs_0_), channel_id=1, source_target_pairs={{0,64},{2,66},{4,68},{6,70},{8,72},{10,74},{12,76},{14,78},{16,80}... | collective-permute-start | bytes 540680 | tf_op jit(solution)/shard_map/ppermute | solution.py:422
  9.0 5.6 %collective-permute-done.refs_1_ = bf16[88,1024]{1,0:T(8,128)(2,1)S(1)} collective-permute-done((bf16[88,1024]{1,0:T(8,128)(2,1)S(1)}, bf16[88,1024]{1,0:T(8,128)(2,1)S(1)}, u32[]{:S(2)}, u32[]{:S(2)}) %collective-permute-start) | collective-permute-done | bytes 180256 | tf_op jit(solution)/shard_map/ppermute | solution.py:422
  14.5 0.0 collective-permute-done.1.refs_3_
  14.5 0.0 collective-permute-done.2.refs_4_
  14.5 0.0 collective-permute-done.3.refs_5_
  14.6 3.0 %collective-permute-start.5 = (bf16[80,1280]{1,0:T(8,128)(2,1)}, bf16[80,1280]{1,0:T(8,128)(2,1)S(1)}, u32[]{:S(2)}, u32[]{:S(2)}) collective-permute-start(bf16[80,1280]{1,0:T(8,128)(2,1)} %param.14), channel_id=1, source_target_pairs={{0,1},{1,0},{2,3},{3,2},{4,5},{5,4},{6,7},{7,6},{8,9},{9,8},{10,11... | collective-permute-start | bytes 614408 | tf_op jit(solution)/shard_map/ppermute | solution.py:431
  17.6 9.8 %collective-permute-start.6 = (bf16[88,1024]{1,0:T(8,128)(2,1)S(1)}, bf16[88,1024]{1,0:T(8,128)(2,1)S(1)}, u32[]{:S(2)}, u32[]{:S(2)}) collective-permute-start(bf16[88,1024]{1,0:T(8,128)(2,1)S(1)} %get-tuple-element.36.refs_0_), channel_id=1, source_target_pairs={{0,160},{2,226},{4,164},{6,230},{8,168},{10,234},{12,172},{14,238}... | collective-permute-start | bytes 540680 | tf_op jit(solution)/shard_map/ppermute | solution.py:422
  27.4 0.0 collective-permute-start.7
  27.4 5.6 %attend_first.1 = (bf16[88,1024]{1,0:T(8,128)(2,1)S(1)}, bf16[88,1024]{1,0:T(8,128)(2,1)S(1)}, bf16[4,1024,80]{2,1,0:T(8,128)(2,1)S(1)}, bf16[4,88,1024]{2,1,0:T(8,128)(2,1)S(1)}) custom-call(bf16[88,1024]{1,0:T(8,128)(2,1)S(1)} %get-tuple-element.36.refs_0_, bf16[88,1024]{1,0:T(8,128)(2,1)S(1)} %collective-permute-done.refs_1_, ...), custom_call_target="tpu_custom_call" | custom-call | tf_op jit(solution)/shard_map/attend_first/pallas_call | solution.py:224
  33.0 0.0 collective-permute-done.5
  33.0 1.0 pad_maximum_fusion.refs_0_
  34.0 0.0 collective-permute-done.6.refs_0_
  34.0 5.2 %collective-permute-done.7.refs_1_ = bf16[88,1024]{1,0:T(8,128)(2,1)S(1)} collective-permute-done((bf16[88,1024]{1,0:T(8,128)(2,1)S(1)}, bf16[88,1024]{1,0:T(8,128)(2,1)S(1)}, u32[]{:S(2)}, u32[]{:S(2)}) %collective-permute-start.7) | collective-permute-done | bytes 180256 | tf_op jit(solution)/shard_map/ppermute | solution.py:422
  39.2 0.2 collective-permute-start.10
  39.4 1.3 %collective-permute-start.11 = (bf16[160,1280]{1,0:T(8,128)(2,1)S(1)}, bf16[160,1280]{1,0:T(8,128)(2,1)S(1)}, u32[]{:S(2)}, u32[]{:S(2)}) collective-permute-start(bf16[160,1280]{1,0:T(8,128)(2,1)S(1)} %pad_maximum_fusion.refs_0_), channel_id=1, source_target_pairs={{0,12},{1,13},{2,14},{3,15},{4,0},{5,1},{6,2},{7,3},{8,4},{9,5},{1... | collective-permute-start | bytes 1228808 | tf_op jit(solution)/shard_map/ppermute | solution.py:431
  40.7 1.1 collective-permute-start.12
  41.8 4.5 %collective-permute-start.4 = (bf16[88,1024]{1,0:T(8,128)(2,1)S(1)}, bf16[88,1024]{1,0:T(8,128)(2,1)S(1)}, u32[]{:S(2)}, u32[]{:S(2)}) collective-permute-start(bf16[88,1024]{1,0:T(8,128)(2,1)S(1)} %get-tuple-element.34), channel_id=1, source_target_pairs={{0,64},{2,66},{4,68},{6,70},{8,72},{10,74},{12,76},{14,78},{16,80}... | collective-permute-start | bytes 540680 | tf_op jit(solution)/shard_map/ppermute | solution.py:422
  46.3 6.8 %attend_next.1 = (bf16[88,1024]{1,0:T(8,128)(2,1)S(1)}, bf16[88,1024]{1,0:T(8,128)(2,1)S(1)}) custom-call(bf16[88,1024]{1,0:T(8,128)(2,1)S(1)} %collective-permute-done.6.refs_0_, bf16[88,1024]{1,0:T(8,128)(2,1)S(1)} %collective-permute-done.7.refs_1_, bf16[4,1024,80]{2,1,0:T(8,128)(2,1)S(1)} %get-tuple-element.41.refs_2_, ...), custom_call_target="tpu_custom_call" | custom-call | tf_op jit(solution)/shard_map/attend_next/pallas_call | solution.py:224
  53.2 3.5 %collective-permute-start.8 = (bf16[88,1024]{1,0:T(8,128)(2,1)S(1)}, bf16[88,1024]{1,0:T(8,128)(2,1)S(1)}, u32[]{:S(2)}, u32[]{:S(2)}) collective-permute-start(bf16[88,1024]{1,0:T(8,128)(2,1)S(1)} %get-tuple-element.43), channel_id=1, source_target_pairs={{0,160},{2,226},{4,164},{6,230},{8,168},{10,234},{12,172},{14,238}... | collective-permute-start | bytes 540680 | tf_op jit(solution)/shard_map/ppermute | solution.py:422
  56.6 0.0 collective-permute-done.10.refs_1_
  56.6 3.1 %collective-permute-start.9 = (bf16[88,1024]{1,0:T(8,128)(2,1)S(1)}, bf16[88,1024]{1,0:T(8,128)(2,1)S(1)}, u32[]{:S(2)}, u32[]{:S(2)}) collective-permute-start(bf16[88,1024]{1,0:T(8,128)(2,1)S(1)} %get-tuple-element.44), channel_id=1, source_target_pairs={{0,224},{2,162},{4,228},{6,166},{8,232},{10,170},{12,236},{14,174}... | collective-permute-start | bytes 540680 | tf_op jit(solution)/shard_map/ppermute | solution.py:422
  59.7 0.7 dynamic-slice_bitcast_fusion.heads
  60.4 0.0 collective-permute-done.11.refs_2_
  60.4 0.0 collective-permute-done.12.refs_3_
  60.4 2.8 %assemble.1.refs_0_ = bf16[640,1280]{1,0:T(8,128)(2,1)S(1)} custom-call(s32[24]{0:T(128)S(1)} %dynamic-slice_bitcast_fusion.heads, bf16[160,1280]{1,0:T(8,128)(2,1)S(1)} %pad_maximum_fusion.refs_0_, bf16[160,1280]{1,0:T(8,128)(2,1)S(1)} %collective-permute-done.10.refs_1_, bf16[160,1280]{1,0:T(8,128)(2,1)S(1)} %collective-permute-done.11.refs_2_, ...), custom_call_target="tpu_custom_call" | custom-call | tf_op jit(solution)/shard_map/assemble/pallas_call | solution.py:293
  63.2 0.0 collective-permute-done.4.refs_1_
  63.2 0.0 collective-permute-done.8.refs_2_
  63.2 1.0 collective-permute-done.9.refs_3_
  64.2 10.3 %collective-permute-start.17 = (bf16[640,1280]{1,0:T(8,128)(2,1)S(1)}, bf16[640,1280]{1,0:T(8,128)(2,1)S(1)}, u32[]{:S(2)}, u32[]{:S(2)}) collective-permute-start(bf16[640,1280]{1,0:T(8,128)(2,1)S(1)} %assemble.1.refs_0_), channel_id=1, source_target_pairs={{0,2},{1,3},{2,0},{3,1},{4,6},{5,7},{6,4},{7,5},{8,10},{9,11},{10,... | collective-permute-start | bytes 4915208 | tf_op jit(solution)/shard_map/ppermute | solution.py:431
  74.5 0.2 combine.1.refs_0_
  74.7 0.1 collective-permute-start.13
  74.8 3.1 %collective-permute-done.13.refs_1_ = bf16[80,1024]{1,0:T(8,128)(2,1)S(1)} collective-permute-done((bf16[80,1024]{1,0:T(8,128)(2,1)S(1)}, bf16[80,1024]{1,0:T(8,128)(2,1)S(1)}, u32[]{:S(2)}, u32[]{:S(2)}) %collective-permute-start.13) | collective-permute-done | bytes 163872 | tf_op jit(solution)/shard_map/ppermute | solution.py:431
  77.9 0.0 copy-start.1
  77.9 0.0 copy-start.2
  77.9 0.0 copy-start.3
  78.0 0.0 copy-start
  78.0 0.9 collective-permute-start.14
  78.9 1.3 %collective-permute-start.15 = (bf16[160,1024]{1,0:T(8,128)(2,1)S(1)}, bf16[160,1024]{1,0:T(8,128)(2,1)S(1)}, u32[]{:S(2)}, u32[]{:S(2)}) collective-permute-start(bf16[160,1024]{1,0:T(8,128)(2,1)S(1)} %pad_maximum_fusion.1), channel_id=1, source_target_pairs={{0,8},{1,9},{2,3},{3,2},{4,12},{5,13},{6,7},{7,6},{8,0},{9,1},{10,... | collective-permute-start | bytes 983048 | tf_op jit(solution)/shard_map/ppermute | solution.py:431
  80.2 2.1 %collective-permute-start.16 = (bf16[160,1024]{1,0:T(8,128)(2,1)S(1)}, bf16[160,1024]{1,0:T(8,128)(2,1)S(1)}, u32[]{:S(2)}, u32[]{:S(2)}) collective-permute-start(bf16[160,1024]{1,0:T(8,128)(2,1)S(1)} %pad_maximum_fusion.1), channel_id=1, source_target_pairs={{0,5},{1,4},{2,15},{3,14},{4,9},{5,8},{6,3},{7,2},{8,13},{9,12},{1... | collective-permute-start | bytes 983048 | tf_op jit(solution)/shard_map/ppermute | solution.py:431
  82.3 3.3 %collective-permute-start.18 = (bf16[80,1024]{1,0:T(8,128)(2,1)S(1)}, bf16[80,1024]{1,0:T(8,128)(2,1)S(1)}, u32[]{:S(2)}, u32[]{:S(2)}) collective-permute-start(bf16[80,1024]{1,0:T(8,128)(2,1)S(1)} %combine.1.refs_0_), channel_id=1, source_target_pairs={{0,9},{1,8},{2,11},{3,10},{4,13},{5,12},{6,15},{7,14},{8,1},{9,0},... | collective-permute-start | bytes 491528 | tf_op jit(solution)/shard_map/ppermute | solution.py:431
  85.6 0.1 collective-permute-done.14.refs_2_
  85.7 4.7 %collective-permute-start.19 = (bf16[160,1024]{1,0:T(8,128)(2,1)S(1)}, bf16[160,1024]{1,0:T(8,128)(2,1)S(1)}, u32[]{:S(2)}, u32[]{:S(2)}) collective-permute-start(bf16[160,1024]{1,0:T(8,128)(2,1)S(1)} %collective-permute-done.14.refs_2_), channel_id=1, source_target_pairs={{0,2},{1,3},{2,0},{3,1},{4,6},{5,7},{6,4},{7,5},{8,10},{9,11},{10,... | collective-permute-start | bytes 983048 | tf_op jit(solution)/shard_map/ppermute | solution.py:431
  90.4 0.0 collective-permute-done.15.refs_3_
  90.4 2.3 %collective-permute-start.20 = (bf16[160,1024]{1,0:T(8,128)(2,1)S(1)}, bf16[160,1024]{1,0:T(8,128)(2,1)S(1)}, u32[]{:S(2)}, u32[]{:S(2)}) collective-permute-start(bf16[160,1024]{1,0:T(8,128)(2,1)S(1)} %collective-permute-done.15.refs_3_), channel_id=1, source_target_pairs={{0,2},{1,3},{2,0},{3,1},{4,6},{5,7},{6,4},{7,5},{8,10},{9,11},{10,... | collective-permute-start | bytes 983048 | tf_op jit(solution)/shard_map/ppermute | solution.py:431
  92.7 1.6 %collective-permute-done.16.refs_4_ = bf16[160,1024]{1,0:T(8,128)(2,1)S(1)} collective-permute-done((bf16[160,1024]{1,0:T(8,128)(2,1)S(1)}, bf16[160,1024]{1,0:T(8,128)(2,1)S(1)}, u32[]{:S(2)}, u32[]{:S(2)}) %collective-permute-start.16) | collective-permute-done | bytes 327712 | tf_op jit(solution)/shard_map/ppermute | solution.py:431
  94.3 4.1 %collective-permute-start.21 = (bf16[160,1024]{1,0:T(8,128)(2,1)S(1)}, bf16[160,1024]{1,0:T(8,128)(2,1)S(1)}, u32[]{:S(2)}, u32[]{:S(2)}) collective-permute-start(bf16[160,1024]{1,0:T(8,128)(2,1)S(1)} %collective-permute-done.16.refs_4_), channel_id=1, source_target_pairs={{0,2},{1,3},{2,0},{3,1},{4,6},{5,7},{6,4},{7,5},{8,10},{9,11},{10,... | collective-permute-start | bytes 983048 | tf_op jit(solution)/shard_map/ppermute | solution.py:431
  98.4 0.0 collective-permute-done.17.refs_1_
  98.4 0.4 join.1.refs_10_
  98.8 0.2 collective-permute-done.18.refs_5_
  99.0 0.2 collective-permute-start.22
  99.1 0.0 copy-done.1
  99.1 0.0 copy-done.2
  99.2 0.0 copy-done.3
  99.2 0.0 collective-permute-done.19.refs_6_
  99.2 0.0 collective-permute-done.20.refs_7_
  99.2 0.4 collective-permute-done.21.refs_8_
  99.6 0.9 collective-permute-done.22.refs_9_
  100.5 0.0 copy-done
  100.5 12.7 %project.1 = bf16[320,256]{1,0:T(8,128)(2,1)} custom-call(s32[24]{0:T(128)S(1)} %dynamic-slice_bitcast_fusion.heads, bf16[80,1024]{1,0:T(8,128)(2,1)S(1)} %combine.1.refs_0_, bf16[80,1024]{1,0:T(8,128)(2,1)S(1)} %collective-permute-done.13.refs_1_, bf16[160,1024]{1,0:T(8,128)(2,1)S(1)} %collective-permute-done.14.refs_2_, ...), custom_call_target="tpu_custom_call" | custom-call | tf_op jit(solution)/shard_map/project/pallas_call | solution.py:367
  (4 shorter events, 0.0 us)
Async XLA Ops:
  1.1 13.4 %collective-permute-start.1 = (bf16[168,1024]{1,0:T(8,128)(2,1)S(1)}, bf16[168,1024]{1,0:T(8,128)(2,1)S(1)}, u32[]{:S(2)}, u32[]{:S(2)}) collective-permute-start(bf16[168,1024]{1,0:T(8,128)(2,1)S(1)} %get-tuple-element.32.refs_2_), channel_id=1, source_target_pairs={{0,16},{2,114},{4,20},{6,118},{8,24},{10,122},{12,28},{14,126},{16... | collective-permute-start | bytes 1032200 | tf_op jit(solution)/shard_map/ppermute | solution.py:422
  1.2 13.3 %collective-permute-start.2 = (bf16[168,1024]{1,0:T(8,128)(2,1)S(1)}, bf16[168,1024]{1,0:T(8,128)(2,1)S(1)}, u32[]{:S(2)}, u32[]{:S(2)}) collective-permute-start(bf16[168,1024]{1,0:T(8,128)(2,1)S(1)} %get-tuple-element.32.refs_2_), channel_id=1, source_target_pairs={{0,128},{2,130},{4,132},{6,134},{8,136},{10,138},{12,140},{14,142}... | collective-permute-start | bytes 1032200 | tf_op jit(solution)/shard_map/ppermute | solution.py:422
  2.6 12.0 %collective-permute-start.3 = (bf16[168,1024]{1,0:T(8,128)(2,1)S(1)}, bf16[168,1024]{1,0:T(8,128)(2,1)S(1)}, u32[]{:S(2)}, u32[]{:S(2)}) collective-permute-start(bf16[168,1024]{1,0:T(8,128)(2,1)S(1)} %get-tuple-element.32.refs_2_), channel_id=1, source_target_pairs={{0,144},{2,242},{4,148},{6,246},{8,152},{10,250},{12,156},{14,254}... | collective-permute-start | bytes 1032200 | tf_op jit(solution)/shard_map/ppermute | solution.py:422
  3.9 10.7 %collective-permute-start = (bf16[88,1024]{1,0:T(8,128)(2,1)S(1)}, bf16[88,1024]{1,0:T(8,128)(2,1)S(1)}, u32[]{:S(2)}, u32[]{:S(2)}) collective-permute-start(bf16[88,1024]{1,0:T(8,128)(2,1)S(1)} %get-tuple-element.36.refs_0_), channel_id=1, source_target_pairs={{0,64},{2,66},{4,68},{6,70},{8,72},{10,74},{12,76},{14,78},{16,80}... | collective-permute-start | bytes 540680 | tf_op jit(solution)/shard_map/ppermute | solution.py:422
  14.6 18.4 %collective-permute-start.5 = (bf16[80,1280]{1,0:T(8,128)(2,1)}, bf16[80,1280]{1,0:T(8,128)(2,1)S(1)}, u32[]{:S(2)}, u32[]{:S(2)}) collective-permute-start(bf16[80,1280]{1,0:T(8,128)(2,1)} %param.14), channel_id=1, source_target_pairs={{0,1},{1,0},{2,3},{3,2},{4,5},{5,4},{6,7},{7,6},{8,9},{9,8},{10,11... | collective-permute-start | bytes 614408 | tf_op jit(solution)/shard_map/ppermute | solution.py:431
  17.6 16.4 %collective-permute-start.6 = (bf16[88,1024]{1,0:T(8,128)(2,1)S(1)}, bf16[88,1024]{1,0:T(8,128)(2,1)S(1)}, u32[]{:S(2)}, u32[]{:S(2)}) collective-permute-start(bf16[88,1024]{1,0:T(8,128)(2,1)S(1)} %get-tuple-element.36.refs_0_), channel_id=1, source_target_pairs={{0,160},{2,226},{4,164},{6,230},{8,168},{10,234},{12,172},{14,238}... | collective-permute-start | bytes 540680 | tf_op jit(solution)/shard_map/ppermute | solution.py:422
  27.4 11.9 %collective-permute-start.7 = (bf16[88,1024]{1,0:T(8,128)(2,1)S(1)}, bf16[88,1024]{1,0:T(8,128)(2,1)S(1)}, u32[]{:S(2)}, u32[]{:S(2)}) collective-permute-start(bf16[88,1024]{1,0:T(8,128)(2,1)S(1)} %get-tuple-element.36.refs_0_), channel_id=1, source_target_pairs={{0,224},{2,162},{4,228},{6,166},{8,232},{10,170},{12,236},{14,174}... | collective-permute-start | bytes 540680 | tf_op jit(solution)/shard_map/ppermute | solution.py:422
  39.2 17.4 %collective-permute-start.10 = (bf16[160,1280]{1,0:T(8,128)(2,1)S(1)}, bf16[160,1280]{1,0:T(8,128)(2,1)S(1)}, u32[]{:S(2)}, u32[]{:S(2)}) collective-permute-start(bf16[160,1280]{1,0:T(8,128)(2,1)S(1)} %pad_maximum_fusion.refs_0_), channel_id=1, source_target_pairs={{0,4},{1,5},{2,6},{3,7},{4,8},{5,9},{6,10},{7,11},{8,12},{9,13},{1... | collective-permute-start | bytes 1228808 | tf_op jit(solution)/shard_map/ppermute | solution.py:431
  39.4 21.0 %collective-permute-start.11 = (bf16[160,1280]{1,0:T(8,128)(2,1)S(1)}, bf16[160,1280]{1,0:T(8,128)(2,1)S(1)}, u32[]{:S(2)}, u32[]{:S(2)}) collective-permute-start(bf16[160,1280]{1,0:T(8,128)(2,1)S(1)} %pad_maximum_fusion.refs_0_), channel_id=1, source_target_pairs={{0,12},{1,13},{2,14},{3,15},{4,0},{5,1},{6,2},{7,3},{8,4},{9,5},{1... | collective-permute-start | bytes 1228808 | tf_op jit(solution)/shard_map/ppermute | solution.py:431
  40.7 19.7 %collective-permute-start.12 = (bf16[160,1280]{1,0:T(8,128)(2,1)S(1)}, bf16[160,1280]{1,0:T(8,128)(2,1)S(1)}, u32[]{:S(2)}, u32[]{:S(2)}) collective-permute-start(bf16[160,1280]{1,0:T(8,128)(2,1)S(1)} %pad_maximum_fusion.refs_0_), channel_id=1, source_target_pairs={{0,8},{1,9},{2,10},{3,11},{4,12},{5,13},{6,14},{7,15},{8,0},{9,1},... | collective-permute-start | bytes 1228808 | tf_op jit(solution)/shard_map/ppermute | solution.py:431
  41.8 21.4 %collective-permute-start.4 = (bf16[88,1024]{1,0:T(8,128)(2,1)S(1)}, bf16[88,1024]{1,0:T(8,128)(2,1)S(1)}, u32[]{:S(2)}, u32[]{:S(2)}) collective-permute-start(bf16[88,1024]{1,0:T(8,128)(2,1)S(1)} %get-tuple-element.34), channel_id=1, source_target_pairs={{0,64},{2,66},{4,68},{6,70},{8,72},{10,74},{12,76},{14,78},{16,80}... | collective-permute-start | bytes 540680 | tf_op jit(solution)/shard_map/ppermute | solution.py:422
  53.2 10.1 %collective-permute-start.8 = (bf16[88,1024]{1,0:T(8,128)(2,1)S(1)}, bf16[88,1024]{1,0:T(8,128)(2,1)S(1)}, u32[]{:S(2)}, u32[]{:S(2)}) collective-permute-start(bf16[88,1024]{1,0:T(8,128)(2,1)S(1)} %get-tuple-element.43), channel_id=1, source_target_pairs={{0,160},{2,226},{4,164},{6,230},{8,168},{10,234},{12,172},{14,238}... | collective-permute-start | bytes 540680 | tf_op jit(solution)/shard_map/ppermute | solution.py:422
  56.6 7.6 %collective-permute-start.9 = (bf16[88,1024]{1,0:T(8,128)(2,1)S(1)}, bf16[88,1024]{1,0:T(8,128)(2,1)S(1)}, u32[]{:S(2)}, u32[]{:S(2)}) collective-permute-start(bf16[88,1024]{1,0:T(8,128)(2,1)S(1)} %get-tuple-element.44), channel_id=1, source_target_pairs={{0,224},{2,162},{4,228},{6,166},{8,232},{10,170},{12,236},{14,174}... | collective-permute-start | bytes 540680 | tf_op jit(solution)/shard_map/ppermute | solution.py:422
  64.2 34.1 %collective-permute-start.17 = (bf16[640,1280]{1,0:T(8,128)(2,1)S(1)}, bf16[640,1280]{1,0:T(8,128)(2,1)S(1)}, u32[]{:S(2)}, u32[]{:S(2)}) collective-permute-start(bf16[640,1280]{1,0:T(8,128)(2,1)S(1)} %assemble.1.refs_0_), channel_id=1, source_target_pairs={{0,2},{1,3},{2,0},{3,1},{4,6},{5,7},{6,4},{7,5},{8,10},{9,11},{10,... | collective-permute-start | bytes 4915208 | tf_op jit(solution)/shard_map/ppermute | solution.py:431
  74.7 3.2 %collective-permute-start.13 = (bf16[80,1024]{1,0:T(8,128)(2,1)S(1)}, bf16[80,1024]{1,0:T(8,128)(2,1)S(1)}, u32[]{:S(2)}, u32[]{:S(2)}) collective-permute-start(bf16[80,1024]{1,0:T(8,128)(2,1)S(1)} %combine.1.refs_0_), channel_id=1, source_target_pairs={{0,2},{1,3},{2,0},{3,1},{4,6},{5,7},{6,4},{7,5},{8,10},{9,11},{10,... | collective-permute-start | bytes 491528 | tf_op jit(solution)/shard_map/ppermute | solution.py:431
  77.9 21.2 %copy-start.1 = (f32[1280]{0:T(1024)S(1)}, f32[1280]{0:T(1024)}, u32[]{:S(2)}) copy-start(f32[1280]{0:T(1024)} %param.15) | copy-start | bytes 15364
  77.9 21.2 %copy-start.2 = (f32[1280]{0:T(1024)S(1)}, f32[1280]{0:T(1024)}, u32[]{:S(2)}) copy-start(f32[1280]{0:T(1024)} %param.16) | copy-start | bytes 15364
  77.9 21.2 %copy-start.3 = (f32[320]{0:T(512)S(1)}, f32[320]{0:T(512)}, u32[]{:S(2)}) copy-start(f32[320]{0:T(512)} %param.18) | copy-start | bytes 3844
  78.0 22.5 %copy-start = (bf16[5120,320]{0,1:T(8,128)(2,1)S(1)}, bf16[5120,320]{0,1:T(8,128)(2,1)}, u32[]{:S(2)}) copy-start(bf16[5120,320]{0,1:T(8,128)(2,1)} %param.17) | copy-start | bytes 9830404
  78.0 7.7 %collective-permute-start.14 = (bf16[160,1024]{1,0:T(8,128)(2,1)S(1)}, bf16[160,1024]{1,0:T(8,128)(2,1)S(1)}, u32[]{:S(2)}, u32[]{:S(2)}) collective-permute-start(bf16[160,1024]{1,0:T(8,128)(2,1)S(1)} %pad_maximum_fusion.1), channel_id=1, source_target_pairs={{0,4},{1,5},{2,14},{3,15},{4,8},{5,9},{6,2},{7,3},{8,12},{9,13},{1... | collective-permute-start | bytes 983048 | tf_op jit(solution)/shard_map/ppermute | solution.py:431
  78.9 11.5 %collective-permute-start.15 = (bf16[160,1024]{1,0:T(8,128)(2,1)S(1)}, bf16[160,1024]{1,0:T(8,128)(2,1)S(1)}, u32[]{:S(2)}, u32[]{:S(2)}) collective-permute-start(bf16[160,1024]{1,0:T(8,128)(2,1)S(1)} %pad_maximum_fusion.1), channel_id=1, source_target_pairs={{0,8},{1,9},{2,3},{3,2},{4,12},{5,13},{6,7},{7,6},{8,0},{9,1},{10,... | collective-permute-start | bytes 983048 | tf_op jit(solution)/shard_map/ppermute | solution.py:431
  80.2 14.1 %collective-permute-start.16 = (bf16[160,1024]{1,0:T(8,128)(2,1)S(1)}, bf16[160,1024]{1,0:T(8,128)(2,1)S(1)}, u32[]{:S(2)}, u32[]{:S(2)}) collective-permute-start(bf16[160,1024]{1,0:T(8,128)(2,1)S(1)} %pad_maximum_fusion.1), channel_id=1, source_target_pairs={{0,5},{1,4},{2,15},{3,14},{4,9},{5,8},{6,3},{7,2},{8,13},{9,12},{1... | collective-permute-start | bytes 983048 | tf_op jit(solution)/shard_map/ppermute | solution.py:431
  82.3 16.7 %collective-permute-start.18 = (bf16[80,1024]{1,0:T(8,128)(2,1)S(1)}, bf16[80,1024]{1,0:T(8,128)(2,1)S(1)}, u32[]{:S(2)}, u32[]{:S(2)}) collective-permute-start(bf16[80,1024]{1,0:T(8,128)(2,1)S(1)} %combine.1.refs_0_), channel_id=1, source_target_pairs={{0,9},{1,8},{2,11},{3,10},{4,13},{5,12},{6,15},{7,14},{8,1},{9,0},... | collective-permute-start | bytes 491528 | tf_op jit(solution)/shard_map/ppermute | solution.py:431
  85.7 13.5 %collective-permute-start.19 = (bf16[160,1024]{1,0:T(8,128)(2,1)S(1)}, bf16[160,1024]{1,0:T(8,128)(2,1)S(1)}, u32[]{:S(2)}, u32[]{:S(2)}) collective-permute-start(bf16[160,1024]{1,0:T(8,128)(2,1)S(1)} %collective-permute-done.14.refs_2_), channel_id=1, source_target_pairs={{0,2},{1,3},{2,0},{3,1},{4,6},{5,7},{6,4},{7,5},{8,10},{9,11},{10,... | collective-permute-start | bytes 983048 | tf_op jit(solution)/shard_map/ppermute | solution.py:431
  90.4 8.8 %collective-permute-start.20 = (bf16[160,1024]{1,0:T(8,128)(2,1)S(1)}, bf16[160,1024]{1,0:T(8,128)(2,1)S(1)}, u32[]{:S(2)}, u32[]{:S(2)}) collective-permute-start(bf16[160,1024]{1,0:T(8,128)(2,1)S(1)} %collective-permute-done.15.refs_3_), channel_id=1, source_target_pairs={{0,2},{1,3},{2,0},{3,1},{4,6},{5,7},{6,4},{7,5},{8,10},{9,11},{10,... | collective-permute-start | bytes 983048 | tf_op jit(solution)/shard_map/ppermute | solution.py:431
  94.3 5.4 %collective-permute-start.21 = (bf16[160,1024]{1,0:T(8,128)(2,1)S(1)}, bf16[160,1024]{1,0:T(8,128)(2,1)S(1)}, u32[]{:S(2)}, u32[]{:S(2)}) collective-permute-start(bf16[160,1024]{1,0:T(8,128)(2,1)S(1)} %collective-permute-done.16.refs_4_), channel_id=1, source_target_pairs={{0,2},{1,3},{2,0},{3,1},{4,6},{5,7},{6,4},{7,5},{8,10},{9,11},{10,... | collective-permute-start | bytes 983048 | tf_op jit(solution)/shard_map/ppermute | solution.py:431
  99.0 1.5 %collective-permute-start.22 = (bf16[80,1024]{1,0:T(8,128)(2,1)S(1)}, bf16[80,1024]{1,0:T(8,128)(2,1)S(1)}, u32[]{:S(2)}, u32[]{:S(2)}) collective-permute-start(bf16[80,1024]{1,0:T(8,128)(2,1)S(1)} %collective-permute-done.18.refs_5_), channel_id=1, source_target_pairs={{0,2},{1,3},{2,0},{3,1},{4,6},{5,7},{6,4},{7,5},{8,10},{9,11},{10,... | collective-permute-start | bytes 491528 | tf_op jit(solution)/shard_map/ppermute | solution.py:431

commit v2 on v1

--- a/solution.py
+++ b/solution.py
@@ -18,7 +18,6 @@
 f32, bf16 = jnp.float32, jnp.bfloat16
 GROUP = ("section", "tp")
 IN_VMEM = pl.BlockSpec(memory_space=pltpu.VMEM)
-IN_SMEM = pl.BlockSpec(memory_space=pltpu.SMEM)
 
 
 def pack_kernel(queries, keys, values, ids, query_block, key_block, held_ids, sems):
@@ -242,8 +241,13 @@
     return list(out[: len(queries)]), list(out[len(queries) :])
 
 
+def this_core():
+    return lax.rem(lax.axis_index("section"), 2)
+
+
 def combine_kernel(*refs):
-    parts, out = refs[:4], refs[4]
+    parts, (mine, others, whole) = refs[:4], refs[4:]
+    core = this_core()
     sums, maxima = [], []
     for part in parts:
         rows = part[80:88, :].astype(f32)
@@ -251,155 +255,119 @@
         maxima.append((rows[2:3, :] + rows[3:4, :]) + rows[4:5, :])
     top = functools.reduce(jnp.maximum, maxima)
     factors = [jnp.exp2((m - top) * EXP2_SCALE) for m in maxima]
-    whole = functools.reduce(jnp.add, [w * s for w, s in zip(factors, sums)])
-    inverse = 1.0 / whole
+    inverse = 1.0 / functools.reduce(jnp.add, [w * s for w, s in zip(factors, sums)])
     mixed = functools.reduce(
         jnp.add, [part[0:80, :].astype(f32) * w for part, w in zip(parts, factors)]
     )
-    out[...] = (mixed * inverse).astype(bf16)
+    whole[...] = (mixed * inverse).astype(bf16)
+    half = mine.shape[1]
+    mine[...] = whole[:, pl.ds(pl.multiple_of(core * half, 128), half)]
+    others[...] = whole[:, pl.ds(pl.multiple_of((1 - core) * half, 128), half)]
 
 
 def combine(parts):
     count = parts[0].shape[1]
     return pl.pallas_call(
         combine_kernel,
-        out_shape=jax.ShapeDtypeStruct((80, count), bf16),
+        out_shape=[jax.ShapeDtypeStruct((80, count // 2), bf16)] * 2,
         in_specs=[IN_VMEM] * 4,
-        out_specs=IN_VMEM,
+        out_specs=[IN_VMEM] * 2,
+        scratch_shapes=[pltpu.VMEM((80, count), bf16)],
         compiler_params=pltpu.CompilerParams(vmem_limit_bytes=6 << 20),
         name="combine",
     )(*parts)
 
 
-def place_heads(heads, at, pieces, whole, sems):
+def copies_kernel(moves, *refs):
+    sources, whole, sems = refs[:-2], refs[-2], refs[-1]
     copies = []
-    for piece in pieces:
-        for i in range(piece.shape[0] // HDIM):
-            row = pl.multiple_of(heads[at + len(copies)] * HDIM, 16)
-            source = piece if piece.shape[0] == HDIM else piece.at[pl.ds(i * HDIM, HDIM), :]
-            copy = pltpu.make_async_copy(source, whole.at[pl.ds(row, HDIM), :], sems.at[len(copies)])
-            copy.start()
-            copies.append(copy)
-    return copies
-
-
-def assemble_kernel(heads, *refs):
-    pieces, whole, sems = refs[:-2], refs[-2], refs[-1]
-    for copy in place_heads(heads, 16, pieces, whole, sems):
-        copy.wait()
-
-
-def assemble(heads, pieces):
-    return pl.pallas_call(
-        assemble_kernel,
-        out_shape=jax.ShapeDtypeStruct((8 * HDIM, pieces[0].shape[1]), bf16),
-        in_specs=[IN_SMEM] + [pl.BlockSpec(memory_space=pl.ANY)] * len(pieces),
-        out_specs=IN_VMEM,
-        scratch_shapes=[pltpu.SemaphoreType.DMA((8,))],
-        compiler_params=pltpu.CompilerParams(vmem_limit_bytes=5 << 20),
-        name="assemble",
-    )(heads, *pieces)
-
-
-def join_kernel(*refs):
-    halves, whole, sems = refs[:-2], refs[-2], refs[-1]
-    rows = halves[0].shape[0]
-    copies = [
-        pltpu.make_async_copy(half, whole.at[pl.ds(i * rows, rows), :], sems.at[i])
-        for i, half in enumerate(halves)
-    ]
-    for copy in copies:
-        copy.start()
+    for i, (source, start, target, rows) in enumerate(moves):
+        copies.append(
+            pltpu.make_async_copy(
+                sources[source].at[start : start + rows, :],
+                whole.at[target : target + rows, :],
+                sems.at[i],
+            )
+        )
+        copies[-1].start()
     for copy in copies:
         copy.wait()
 
 
-def join(halves):
-    rows, width = halves[0].shape
+def place_rows(sources, moves, name):
+    rows = sum(move[3] for move in moves)
     return pl.pallas_call(
-        join_kernel,
-        out_shape=jax.ShapeDtypeStruct((len(halves) * rows, width), bf16),
-        in_specs=[pl.BlockSpec(memory_space=pl.ANY)] * len(halves),
+        functools.partial(copies_kernel, moves),
+        out_shape=jax.ShapeDtypeStruct((rows, sources[0].shape[1]), bf16),
+        in_specs=[pl.BlockSpec(memory_space=pl.ANY)] * len(sources),
         out_specs=IN_VMEM,
-        scratch_shapes=[pltpu.SemaphoreType.DMA((len(halves),))],
+        scratch_shapes=[pltpu.SemaphoreType.DMA((len(moves),))],
         compiler_params=pltpu.CompilerParams(vmem_limit_bytes=5 << 20),
-        name="join",
-    )(*halves)
-
-
-def project_kernel(count, heads, *refs):
-    pieces = refs[:10]
-    (weight, gain, shift, proj, proj_bias, out, attended, normed, sems) = refs[10:]
-    copies = place_heads(heads, 0, pieces, attended, sems)
+        name=name,
+    )(*sources)
+
+
+def project_kernel(*refs):
+    pieces = refs[:8]
+    (weight, gain, shift, *projs, out_mine, out_others, normed) = refs[8:]
     width = weight.shape[1]
-    step = 512
-    bias_column = jnp.broadcast_to(proj_bias[...], (8, proj.shape[0])).T[:, 0:1]
-    for copy in copies:
-        copy.wait()
-    for b in range(count // step):
-        turned = attended[:, b * step : (b + 1) * step].T
-        rows = jnp.dot(turned, weight[...], preferred_element_type=f32).astype(bf16).astype(f32)
-        rows = rows - jnp.sum(rows, axis=1, keepdims=True) * (1.0 / width)
-        spread = jnp.sum(rows * rows, axis=1, keepdims=True) * (1.0 / width)
-        rows = rows * lax.rsqrt(spread + EPSILON) * gain[...] + shift[...]
-        for k in range(width // 128):
-            normed[b, k] = rows[:, k * 128 : (k + 1) * 128]
-        linear = jnp.zeros((proj.shape[0], step // 4), f32)
+    count = pieces[0].shape[1]
+    attended = jnp.concatenate([piece[...] for piece in pieces], axis=0)
+    rows = jnp.dot(attended.T, weight[...], preferred_element_type=f32).astype(bf16).astype(f32)
+    rows = rows - jnp.sum(rows, axis=1, keepdims=True) * (1.0 / width)
+    spread = jnp.sum(rows * rows, axis=1, keepdims=True) * (1.0 / width)
+    rows = rows * lax.rsqrt(spread + EPSILON) * gain[...] + shift[...]
+    for k in range(width // 128):
+        normed[k] = rows[:, k * 128 : (k + 1) * 128]
+    tokens = []
+    for r in range(4):
+        every_fourth = pl.ds(r, count // 4, stride=4)
+        tokens.append(
+            jnp.concatenate(
+                [normed[k, every_fourth, :].astype(bf16) for k in range(width // 128)], axis=1
+            )
+        )
+    for out, proj, bias in ((out_others, projs[2], projs[3]), (out_mine, projs[0], projs[1])):
+        linear = jnp.broadcast_to(bias[...], (8, proj.shape[0])).T[:, 0:1]
         for r in range(4):
-            every_fourth = pl.ds(r, step // 4, stride=4)
-            tokens = jnp.concatenate(
-                [normed[b, k, every_fourth, :].astype(bf16) for k in range(width // 128)], axis=1
-            )
             linear = linear + lax.dot_general(
                 proj[:, r * width : (r + 1) * width],
-                tokens,
+                tokens[r],
                 (((1,), (1,)), ((), ())),
                 preferred_element_type=f32,
             )
-        linear = linear + bias_column
-        active = 0.5 * linear * (1.0 + lax.erf(linear * (0.5**0.5)))
-        out[:, b * (step // 4) : (b + 1) * (step // 4)] = active.astype(bf16)
-
-
-def project(heads, pieces, weight, gain, shift, proj, proj_bias):
-    count = pieces[0].shape[1]
-    depth, width = weight.shape
+        out[...] = (0.5 * linear * (1.0 + lax.erf(linear * (0.5**0.5)))).astype(bf16)
+
+
+def project(pieces, weight, gain, shift, mine, others):
+    count, width = pieces[0].shape[1], weight.shape[1]
     return pl.pallas_call(
-        functools.partial(project_kernel, count),
-        out_shape=jax.ShapeDtypeStruct((proj.shape[0], count // 4), bf16),
-        in_specs=[IN_SMEM] + [pl.BlockSpec(memory_space=pl.ANY)] * 10 + [IN_VMEM] * 5,
+        project_kernel,
+        out_shape=[jax.ShapeDtypeStruct((mine[0].shape[0], count // 4), bf16)] * 2,
+        in_specs=[IN_VMEM] * 15,
+        out_specs=[IN_VMEM] * 2,
+        scratch_shapes=[pltpu.VMEM((width // 128, count, 128), f32)],
+        compiler_params=pltpu.CompilerParams(vmem_limit_bytes=24 << 20),
+        name="project",
+    )(*pieces, weight, gain, shift, *mine, *others)
+
+
+def finish_kernel(mine, rest, out):
+    core, count = this_core(), mine.shape[1]
+    out[:, pl.ds(pl.multiple_of(core * count, 128), count)] = mine[...]
+    out[:, pl.ds(pl.multiple_of((1 - core) * count, 128), count)] = rest[...]
+
+
+def finish(mine, rest):
+    rows, count = mine.shape
+    return pl.pallas_call(
+        finish_kernel,
+        out_shape=jax.ShapeDtypeStruct((rows, 2 * count), bf16),
+        in_specs=[IN_VMEM] * 2,
         out_specs=IN_VMEM,
-        scratch_shapes=[
-            pltpu.VMEM((depth, count), bf16),
-            pltpu.VMEM((count // 512, width // 128, 512, 128), f32),
-            pltpu.SemaphoreType.DMA((16,)),
-        ],
-        compiler_params=pltpu.CompilerParams(vmem_limit_bytes=30 << 20),
-        name="project",
-    )(heads, *pieces, weight, gain, shift, proj, proj_bias)
-
-
-def head_order():
-    table = []
-    for x in range(4):
-        for c in range(2):
-            for t in range(2):
-
-                def slot(a, d, b):
-                    return (d != c) * 8 + a % 4 * 2 + b
-
-                row = [slot(x, c, t), slot(x, 1 - c, t)]
-                for d in (c, 1 - c):
-                    side = x + (3, 1)[d]
-                    cross = (x + 2, t) if d == 0 else (x, 1 - t)
-                    row += [slot(side, d, t), slot(side, 1 - d, t)]
-                    row += [slot(cross[0], d, cross[1]), slot(cross[0], 1 - d, cross[1])]
-                    row += [slot(side, d, 1 - t), slot(side, 1 - d, 1 - t)]
-                    row += [slot(x + 2, d, 1 - t)]
-                for a in (x, x + 3, x + 1, x + 2):
-                    row += [slot(a, c, t), slot(a, c, 1 - t)]
-                table.append(row)
-    return table
+        compiler_params=pltpu.CompilerParams(vmem_limit_bytes=4 << 20),
+        name="finish",
+    )(mine, rest)
 
 
 def on_device(
@@ -430,61 +398,49 @@
                     perm.append(((x * 2 + c) * 2 + t, (a % 4 * 2 + b) * 2 + d))
         return lax.ppermute(block, GROUP, perm)
 
-    me = lax.axis_index("section") * 2 + lax.axis_index("tp")
-    heads = jnp.asarray(head_order(), jnp.int32)[me]
-
     def across(x, c, t):
         return x, 1 - c, t
 
     key_blocks = [swap(key_block, mask) for mask in KEY_PARTNERS]
     queries_at = [query_block, swap(query_block, QUERY_PARTNERS[1])]
-    late_query, late_weight, _ = lax.optimization_barrier(
-        (query_block, out_weight, (key_blocks, queries_at[1]))
+    late_query, late_weight, late_proj, late_bias, _ = lax.optimization_barrier(
+        (query_block, out_weight, proj_weight, proj_bias, (key_blocks, queries_at[1]))
     )
     queries_at += [swap(late_query, mask) for mask in QUERY_PARTNERS[2:]]
     far = send(late_weight, lambda x, c, t: (x, c, 1 - t))
+    mine = (late_proj.T, late_bias[None, :])
+    others = tuple(send(block, across) for block in mine)
     returned, held = attend(queries_at[:2], key_blocks)
-    both = jnp.concatenate([late_weight, far], axis=0)
+    both = place_rows([late_weight, far], [(i, 0, i * HDIM, HDIM) for i in range(2)], "both")
     returned[1] = swap(returned[1], QUERY_PARTNERS[1])
-    both, late_queries, held = lax.optimization_barrier((both, queries_at[2:], held))
-    weights = [both] + [send(both, lambda x, c, t, d=d: (x + d, c, t)) for d in (1, 3, 2)]
+    both, others, late_queries, held = lax.optimization_barrier((both, others, queries_at[2:], held))
+    steps = (1, 3, 2)
+    weights = [both] + [send(both, lambda x, c, t, d=d: (x + d, c, t)) for d in steps]
     late, _ = attend(late_queries, None, held)
     returned += [swap(part, mask) for part, mask in zip(late, QUERY_PARTNERS[2:])]
     weights, late = lax.optimization_barrier((weights, late))
-    half = assemble(heads, weights)
+    half = place_rows(weights, [(i, 0, i * 160, 160) for i in range(4)], "assemble")
     returned, half = lax.optimization_barrier((returned, half))
     other_half = send(half, across)
-    attended = combine(returned)
-
-    def along(x, c, t):
-        return x + (1, -1)[c], c, t
-
-    def along_far(x, c, t):
-        return x + (1, -1)[c], c, 1 - t
-
-    def opposite(x, c, t):
-        return (x + 2, c, t) if c == 0 else (x, c, 1 - t)
-
-    def opposite_far(x, c, t):
-        return x + 2, c, 1 - t
-
-    sibling = send(attended, across)
-    pair = jnp.concatenate([attended, sibling], axis=0)
-    received = [send(pair, along), send(pair, opposite), send(pair, along_far)]
-    received.append(send(attended, opposite_far))
-    weight, received[-1] = lax.optimization_barrier((join([half, other_half]), received[-1]))
-    forwarded = [send(block, across) for block in received]
-    pieces = [attended, sibling] + received + forwarded
-    projected = project(
-        heads,
-        pieces,
+    kept, given = combine(returned)
+
+    pair = place_rows([kept, send(given, across)], [(i, 0, i * HDIM, HDIM) for i in range(2)], "pair")
+    pieces = {(0, 0): pair}
+    for d, e in ((2, 1), (1, 1), (3, 1), (2, 0), (0, 1), (1, 0), (3, 0)):
+        pieces[d, e] = send(pair, lambda x, c, t: (x + d, c, (t + e) % 2))
+    order = [(d, e) for d in (0,) + steps for e in (0, 1)]
+    moves = [(h, i * HDIM, (2 * i + h) * HDIM, HDIM) for i in range(8) for h in range(2)]
+    weight = place_rows([half, other_half], moves, "join")
+    weight, pieces[3, 0] = lax.optimization_barrier((weight, pieces[3, 0]))
+    out_mine, out_others = project(
+        [pieces[place] for place in order],
         weight,
         norm_gain[None, :],
         norm_bias[None, :],
-        proj_weight.T,
-        proj_bias[None, :],
+        mine,
+        others,
     )
-    return projected.T
+    return finish(out_mine, send(out_others, across)).T
 
 
 def solution(mesh):

time: 114 us -> 114 us (level)
  starting transfers between devices: 63.5 us -> 49.6 us
  Pallas kernels: 29.7 us -> 41.4 us
  waiting for transfers between devices: 18.1 us -> 20.6 us
    pallas_call x2, Pallas kernels: 12.5 us -> 29 us  [attend(): pl.pallas_call(functools.partial(attend_kernel, len(queries), first), out...]
    ppermute x9, starting transfers between devices: 28.7 us -> 13.5 us  [swap(): return lax.ppermute(block, ('blk', 'section'), perm)]
    pallas_call x4 -> x7, Pallas kernels: 16.1 us -> 11.3 us  [the longest x4 5.97 us: place_rows(): pl.pallas_call(functools.partial(copies_kernel, moves), out_shape=jax.Sha...]
    ppermute x14 -> x16, waiting for transfers between devices: 6.24 us -> 10.5 us  [send(): return lax.ppermute(block, GROUP, perm)]
    ppermute x9, waiting for transfers between devices: 11.8 us -> 10.1 us  [swap(): return lax.ppermute(block, ('blk', 'section'), perm)]
    ppermute x14 -> x16, starting transfers between devices: 34.8 us -> 36.1 us  [send(): return lax.ppermute(block, GROUP, perm)]
  transfers between devices with their start and end apart: 23 -> 25, of which waited for: 9 -> 7; matrix products, arithmetic and copies ran while one was open for 1% -> 1% of each run, Pallas kernels for 14% -> 31%
where the time goes in v2:
time: 114 us; the launch traced here: 113 us
  starting transfers between devices  49.6 us (44%)
  Pallas kernels  41.4 us (36%)
  waiting for transfers between devices  20.6 us (18%)
  local copies, waits for them, and re-layouts  1.64 us (1%)
    ppermute x16, starting transfers between devices, send(): return lax.ppermute(block, GROUP, perm)  36.1 us
    pallas_call x2, Pallas kernels, attend(): pl.pallas_call(functools.partial(attend_kernel, len(queries), first), out...  29 us
    ppermute x9, starting transfers between devices, swap(): return lax.ppermute(block, ('blk', 'section'), perm)  13.5 us
    ppermute x16, waiting for transfers between devices, send(): return lax.ppermute(block, GROUP, perm)  10.5 us
    ppermute x9, waiting for transfers between devices, swap(): return lax.ppermute(block, ('blk', 'section'), perm)  10.1 us
    pallas_call x4, Pallas kernels, place_rows(): pl.pallas_call(functools.partial(copies_kernel, moves), out_shape=jax.Sha...  5.97 us
    pallas_call x1, Pallas kernels, project(): pl.pallas_call(project_kernel, out_shape=[jax.ShapeDtypeStruct((mine[0].s...  4.4 us
  transfers between devices with their start and end apart: 25, of which 7 were waited for; matrix products, arithmetic and copies ran while one was open for 1% of the time, Pallas kernels for 31%

profile of v2, /device:TPU:71, one launch (start us, length us, event | category | flops | bytes accessed | tf_op | source)
XLA Modules:
  0.0 113.4 jit_solution(8478784937223591158)
XLA Ops:
  0.0 1.1 pack.1
  1.1 0.1 collective-permute-start.1
  1.2 1.4 %collective-permute-start.2 = (bf16[168,1024]{1,0:T(8,128)(2,1)S(1)}, bf16[168,1024]{1,0:T(8,128)(2,1)S(1)}, u32[]{:S(2)}, u32[]{:S(2)}) collective-permute-start(bf16[168,1024]{1,0:T(8,128)(2,1)S(1)} %get-tuple-element.40.refs_2_), channel_id=1, source_target_pairs={{0,128},{2,130},{4,132},{6,134},{8,136},{10,138},{12,140},{14,142}... | collective-permute-start | bytes 1032200 | tf_op jit(solution)/shard_map/ppermute | solution.py:390
  2.6 1.3 %collective-permute-start.3 = (bf16[168,1024]{1,0:T(8,128)(2,1)S(1)}, bf16[168,1024]{1,0:T(8,128)(2,1)S(1)}, u32[]{:S(2)}, u32[]{:S(2)}) collective-permute-start(bf16[168,1024]{1,0:T(8,128)(2,1)S(1)} %get-tuple-element.40.refs_2_), channel_id=1, source_target_pairs={{0,144},{2,242},{4,148},{6,246},{8,152},{10,250},{12,156},{14,254}... | collective-permute-start | bytes 1032200 | tf_op jit(solution)/shard_map/ppermute | solution.py:390
  3.9 5.1 %collective-permute-start = (bf16[88,1024]{1,0:T(8,128)(2,1)S(1)}, bf16[88,1024]{1,0:T(8,128)(2,1)S(1)}, u32[]{:S(2)}, u32[]{:S(2)}) collective-permute-start(bf16[88,1024]{1,0:T(8,128)(2,1)S(1)} %get-tuple-element.46.refs_0_), channel_id=1, source_target_pairs={{0,64},{2,66},{4,68},{6,70},{8,72},{10,74},{12,76},{14,78},{16,80}... | collective-permute-start | bytes 540680 | tf_op jit(solution)/shard_map/ppermute | solution.py:390
  9.0 5.6 %collective-permute-done.refs_1_ = bf16[88,1024]{1,0:T(8,128)(2,1)S(1)} collective-permute-done((bf16[88,1024]{1,0:T(8,128)(2,1)S(1)}, bf16[88,1024]{1,0:T(8,128)(2,1)S(1)}, u32[]{:S(2)}, u32[]{:S(2)}) %collective-permute-start) | collective-permute-done | bytes 180256 | tf_op jit(solution)/shard_map/ppermute | solution.py:390
  14.5 0.0 collective-permute-done.1.refs_3_
  14.5 0.0 collective-permute-done.2.refs_4_
  14.5 0.0 collective-permute-done.3.refs_5_
  14.6 10.6 %collective-permute-start.6 = (bf16[320,5120]{1,0:T(8,128)(2,1)}, bf16[320,5120]{1,0:T(8,128)(2,1)S(1)}, u32[]{:S(2)}, u32[]{:S(2)}) collective-permute-start(bf16[320,5120]{1,0:T(8,128)(2,1)} %bitcast.6), channel_id=1, source_target_pairs={{0,2},{1,3},{2,0},{3,1},{4,6},{5,7},{6,4},{7,5},{8,10},{9,11},{10,... | collective-permute-start | bytes 9830408 | tf_op jit(solution)/shard_map/ppermute | solution.py:399
  25.2 2.9 %collective-permute-start.5 = (bf16[80,1280]{1,0:T(8,128)(2,1)}, bf16[80,1280]{1,0:T(8,128)(2,1)S(1)}, u32[]{:S(2)}, u32[]{:S(2)}) collective-permute-start(bf16[80,1280]{1,0:T(8,128)(2,1)} %refs_0_), channel_id=1, source_target_pairs={{0,1},{1,0},{2,3},{3,2},{4,5},{5,4},{6,7},{7,6},{8,9},{9,8},{10,11... | collective-permute-start | bytes 614408 | tf_op jit(solution)/shard_map/ppermute | solution.py:399
  28.1 0.0 collective-permute-start.8
  28.1 2.4 %collective-permute-start.9 = (bf16[88,1024]{1,0:T(8,128)(2,1)S(1)}, bf16[88,1024]{1,0:T(8,128)(2,1)S(1)}, u32[]{:S(2)}, u32[]{:S(2)}) collective-permute-start(bf16[88,1024]{1,0:T(8,128)(2,1)S(1)} %get-tuple-element.46.refs_0_), channel_id=1, source_target_pairs={{0,224},{2,162},{4,228},{6,166},{8,232},{10,170},{12,236},{14,174}... | collective-permute-start | bytes 540680 | tf_op jit(solution)/shard_map/ppermute | solution.py:390
  30.5 0.7 broadcast_in_dim.13.refs_12_
  31.2 0.9 collective-permute-start.7
  32.1 21.4 %attend_first.1 = (bf16[88,1024]{1,0:T(8,128)(2,1)S(1)}, bf16[88,1024]{1,0:T(8,128)(2,1)S(1)}, bf16[4,1024,80]{2,1,0:T(8,128)(2,1)S(1)}, bf16[4,88,1024]{2,1,0:T(8,128)(2,1)S(1)}) custom-call(bf16[88,1024]{1,0:T(8,128)(2,1)S(1)} %get-tuple-element.46.refs_0_, bf16[88,1024]{1,0:T(8,128)(2,1)S(1)} %collective-permute-done.refs_1_, ...), custom_call_target="tpu_custom_call" | custom-call | tf_op jit(solution)/shard_map/attend_first/pallas_call | solution.py:223
  53.5 0.0 collective-permute-done.5.refs_1_
  53.5 0.0 copy-start.1
  53.5 0.9 copy-done.1
  54.5 0.5 both.1.refs_0_
  55.0 0.0 copy-start.2
  55.0 0.0 copy-start.3
  55.0 0.0 collective-permute-done.7.refs_14_
  55.0 0.0 collective-permute-done.8.refs_0_
  55.0 0.0 collective-permute-done.9.refs_1_
  55.0 0.0 collective-permute-done.6.refs_13_
  55.0 0.2 collective-permute-start.12
  55.3 1.3 %collective-permute-start.13 = (bf16[160,1280]{1,0:T(8,128)(2,1)S(1)}, bf16[160,1280]{1,0:T(8,128)(2,1)S(1)}, u32[]{:S(2)}, u32[]{:S(2)}) collective-permute-start(bf16[160,1280]{1,0:T(8,128)(2,1)S(1)} %both.1.refs_0_), channel_id=1, source_target_pairs={{0,12},{1,13},{2,14},{3,15},{4,0},{5,1},{6,2},{7,3},{8,4},{9,5},{1... | collective-permute-start | bytes 1228808 | tf_op jit(solution)/shard_map/ppermute | solution.py:399
  56.6 1.1 collective-permute-start.14
  57.7 0.0 collective-permute-start.4
  57.7 7.6 %attend_next.1 = (bf16[88,1024]{1,0:T(8,128)(2,1)S(1)}, bf16[88,1024]{1,0:T(8,128)(2,1)S(1)}) custom-call(bf16[88,1024]{1,0:T(8,128)(2,1)S(1)} %collective-permute-done.8.refs_0_, bf16[88,1024]{1,0:T(8,128)(2,1)S(1)} %collective-permute-done.9.refs_1_, bf16[4,1024,80]{2,1,0:T(8,128)(2,1)S(1)} %get-tuple-element.51.refs_2_, ...), custom_call_target="tpu_custom_call" | custom-call | tf_op jit(solution)/shard_map/attend_next/pallas_call | solution.py:223
  65.3 0.1 collective-permute-start.10
  65.4 0.0 collective-permute-done.12.refs_1_
  65.4 3.2 %collective-permute-start.11 = (bf16[88,1024]{1,0:T(8,128)(2,1)S(1)}, bf16[88,1024]{1,0:T(8,128)(2,1)S(1)}, u32[]{:S(2)}, u32[]{:S(2)}) collective-permute-start(bf16[88,1024]{1,0:T(8,128)(2,1)S(1)} %get-tuple-element.54), channel_id=1, source_target_pairs={{0,224},{2,162},{4,228},{6,166},{8,232},{10,170},{12,236},{14,174}... | collective-permute-start | bytes 540680 | tf_op jit(solution)/shard_map/ppermute | solution.py:390
  68.6 2.3 %collective-permute-done.13.refs_2_ = bf16[160,1280]{1,0:T(8,128)(2,1)S(1)} collective-permute-done((bf16[160,1280]{1,0:T(8,128)(2,1)S(1)}, bf16[160,1280]{1,0:T(8,128)(2,1)S(1)}, u32[]{:S(2)}, u32[]{:S(2)}) %collective-permute-start.13) | collective-permute-done | bytes 409632 | tf_op jit(solution)/shard_map/ppermute | solution.py:399
  70.9 0.0 collective-permute-done.14.refs_3_
  70.9 0.9 assemble.1.refs_0_
  71.7 0.0 collective-permute-done.4.refs_1_
  71.8 4.5 %collective-permute-done.10.refs_2_ = bf16[88,1024]{1,0:T(8,128)(2,1)S(1)} collective-permute-done((bf16[88,1024]{1,0:T(8,128)(2,1)S(1)}, bf16[88,1024]{1,0:T(8,128)(2,1)S(1)}, u32[]{:S(2)}, u32[]{:S(2)}) %collective-permute-start.10) | collective-permute-done | bytes 180256 | tf_op jit(solution)/shard_map/ppermute | solution.py:390
  76.2 0.0 collective-permute-done.11.refs_3_
  76.2 0.0 collective-permute-start.19
  76.3 0.2 combine.1
  76.5 0.6 collective-permute-start.15
  77.1 2.8 %collective-permute-done.15.refs_1_ = bf16[80,512]{1,0:T(8,128)(2,1)S(1)} collective-permute-done((bf16[80,512]{1,0:T(8,128)(2,1)S(1)}, bf16[80,512]{1,0:T(8,128)(2,1)S(1)}, u32[]{:S(2)}, u32[]{:S(2)}) %collective-permute-start.15) | collective-permute-done | bytes 81952 | tf_op jit(solution)/shard_map/ppermute | solution.py:399
  79.9 0.2 pair.1.refs_0_
  80.1 2.7 %collective-permute-start.16 = (bf16[160,512]{1,0:T(8,128)(2,1)S(1)}, bf16[160,512]{1,0:T(8,128)(2,1)S(1)}, u32[]{:S(2)}, u32[]{:S(2)}) collective-permute-start(bf16[160,512]{1,0:T(8,128)(2,1)S(1)} %pair.1.refs_0_), channel_id=1, source_target_pairs={{0,1},{1,0},{2,3},{3,2},{4,5},{5,4},{6,7},{7,6},{8,9},{9,8},{10,11... | collective-permute-start | bytes 491528 | tf_op jit(solution)/shard_map/ppermute | solution.py:399
  82.7 1.8 %collective-permute-start.20 = (bf16[160,512]{1,0:T(8,128)(2,1)S(1)}, bf16[160,512]{1,0:T(8,128)(2,1)S(1)}, u32[]{:S(2)}, u32[]{:S(2)}) collective-permute-start(bf16[160,512]{1,0:T(8,128)(2,1)S(1)} %pair.1.refs_0_), channel_id=1, source_target_pairs={{0,12},{1,13},{2,14},{3,15},{4,0},{5,1},{6,2},{7,3},{8,4},{9,5},{1... | collective-permute-start | bytes 491528 | tf_op jit(solution)/shard_map/ppermute | solution.py:399
  84.5 0.9 collective-permute-start.17
  85.4 3.0 %collective-permute-start.18 = (bf16[160,512]{1,0:T(8,128)(2,1)S(1)}, bf16[160,512]{1,0:T(8,128)(2,1)S(1)}, u32[]{:S(2)}, u32[]{:S(2)}) collective-permute-start(bf16[160,512]{1,0:T(8,128)(2,1)S(1)} %pair.1.refs_0_), channel_id=1, source_target_pairs={{0,5},{1,4},{2,7},{3,6},{4,9},{5,8},{6,11},{7,10},{8,13},{9,12},{1... | collective-permute-start | bytes 491528 | tf_op jit(solution)/shard_map/ppermute | solution.py:399
  88.4 0.0 collective-permute-done.16.refs_1_
  88.4 3.0 %collective-permute-start.21 = (bf16[160,512]{1,0:T(8,128)(2,1)S(1)}, bf16[160,512]{1,0:T(8,128)(2,1)S(1)}, u32[]{:S(2)}, u32[]{:S(2)}) collective-permute-start(bf16[160,512]{1,0:T(8,128)(2,1)S(1)} %pair.1.refs_0_), channel_id=1, source_target_pairs={{0,13},{1,12},{2,15},{3,14},{4,1},{5,0},{6,3},{7,2},{8,5},{9,4},{1... | collective-permute-start | bytes 491528 | tf_op jit(solution)/shard_map/ppermute | solution.py:399
  91.4 1.4 %collective-permute-start.22 = (bf16[160,512]{1,0:T(8,128)(2,1)S(1)}, bf16[160,512]{1,0:T(8,128)(2,1)S(1)}, u32[]{:S(2)}, u32[]{:S(2)}) collective-permute-start(bf16[160,512]{1,0:T(8,128)(2,1)S(1)} %pair.1.refs_0_), channel_id=1, source_target_pairs={{0,8},{1,9},{2,10},{3,11},{4,12},{5,13},{6,14},{7,15},{8,0},{9,1},... | collective-permute-start | bytes 491528 | tf_op jit(solution)/shard_map/ppermute | solution.py:399
  92.7 0.0 collective-permute-done.19.refs_1_
  92.7 3.9 %collective-permute-start.23 = (bf16[160,512]{1,0:T(8,128)(2,1)S(1)}, bf16[160,512]{1,0:T(8,128)(2,1)S(1)}, u32[]{:S(2)}, u32[]{:S(2)}) collective-permute-start(bf16[160,512]{1,0:T(8,128)(2,1)S(1)} %pair.1.refs_0_), channel_id=1, source_target_pairs={{0,9},{1,8},{2,11},{3,10},{4,13},{5,12},{6,15},{7,14},{8,1},{9,0},... | collective-permute-start | bytes 491528 | tf_op jit(solution)/shard_map/ppermute | solution.py:399
  96.7 0.0 copy-start
  96.7 4.4 %join.1.refs_8_ = bf16[1280,1280]{1,0:T(8,128)(2,1)S(1)} custom-call(bf16[640,1280]{1,0:T(8,128)(2,1)S(1)} %assemble.1.refs_0_, bf16[640,1280]{1,0:T(8,128)(2,1)S(1)} %collective-permute-done.19.refs_1_), custom_call_target="tpu_custom_call" | custom-call | tf_op jit(solution)/shard_map/join/pallas_call | solution.py:299
  101.1 0.0 collective-permute-done.17.refs_2_
  101.2 0.0 collective-permute-done.21.refs_5_
  101.2 0.1 collective-permute-done.22.refs_6_
  101.2 4.4 %collective-permute-done.23.refs_7_ = bf16[160,512]{1,0:T(8,128)(2,1)S(1)} collective-permute-done((bf16[160,512]{1,0:T(8,128)(2,1)S(1)}, bf16[160,512]{1,0:T(8,128)(2,1)S(1)}, u32[]{:S(2)}, u32[]{:S(2)}) %collective-permute-start.23) | collective-permute-done | bytes 163872 | tf_op jit(solution)/shard_map/ppermute | solution.py:399
  105.6 4.4 %project.1 = (bf16[320,128]{1,0:T(8,128)(2,1)S(1)}, bf16[320,128]{1,0:T(8,128)(2,1)S(1)}) custom-call(bf16[160,512]{1,0:T(8,128)(2,1)S(1)} %pair.1.refs_0_, bf16[160,512]{1,0:T(8,128)(2,1)S(1)} %collective-permute-done.16.refs_1_, bf16[160,512]{1,0:T(8,128)(2,1)S(1)} %collective-permute-done.17.refs_2_, ...), custom_call_target="tpu_custom_call" | custom-call | tf_op jit(solution)/shard_map/project/pallas_call | solution.py:344
  110.0 1.8 %collective-permute-start.24 = (bf16[320,128]{1,0:T(8,128)(2,1)S(1)}, bf16[320,128]{1,0:T(8,128)(2,1)S(1)}, u32[]{:S(2)}, u32[]{:S(2)}) collective-permute-start(bf16[320,128]{1,0:T(8,128)(2,1)S(1)} %get-tuple-element.72), channel_id=1, source_target_pairs={{0,2},{1,3},{2,0},{3,1},{4,6},{5,7},{6,4},{7,5},{8,10},{9,11},{10,... | collective-permute-start | bytes 245768 | tf_op jit(solution)/shard_map/ppermute | solution.py:399
  111.8 0.9 collective-permute-done.24.rest
  112.7 0.7 finish.1
  (7 shorter events, 0.0 us)
Async XLA Ops:
  1.1 13.4 %collective-permute-start.1 = (bf16[168,1024]{1,0:T(8,128)(2,1)S(1)}, bf16[168,1024]{1,0:T(8,128)(2,1)S(1)}, u32[]{:S(2)}, u32[]{:S(2)}) collective-permute-start(bf16[168,1024]{1,0:T(8,128)(2,1)S(1)} %get-tuple-element.40.refs_2_), channel_id=1, source_target_pairs={{0,16},{2,114},{4,20},{6,118},{8,24},{10,122},{12,28},{14,126},{16... | collective-permute-start | bytes 1032200 | tf_op jit(solution)/shard_map/ppermute | solution.py:390
  1.2 13.3 %collective-permute-start.2 = (bf16[168,1024]{1,0:T(8,128)(2,1)S(1)}, bf16[168,1024]{1,0:T(8,128)(2,1)S(1)}, u32[]{:S(2)}, u32[]{:S(2)}) collective-permute-start(bf16[168,1024]{1,0:T(8,128)(2,1)S(1)} %get-tuple-element.40.refs_2_), channel_id=1, source_target_pairs={{0,128},{2,130},{4,132},{6,134},{8,136},{10,138},{12,140},{14,142}... | collective-permute-start | bytes 1032200 | tf_op jit(solution)/shard_map/ppermute | solution.py:390
  2.6 12.0 %collective-permute-start.3 = (bf16[168,1024]{1,0:T(8,128)(2,1)S(1)}, bf16[168,1024]{1,0:T(8,128)(2,1)S(1)}, u32[]{:S(2)}, u32[]{:S(2)}) collective-permute-start(bf16[168,1024]{1,0:T(8,128)(2,1)S(1)} %get-tuple-element.40.refs_2_), channel_id=1, source_target_pairs={{0,144},{2,242},{4,148},{6,246},{8,152},{10,250},{12,156},{14,254}... | collective-permute-start | bytes 1032200 | tf_op jit(solution)/shard_map/ppermute | solution.py:390
  3.9 10.7 %collective-permute-start = (bf16[88,1024]{1,0:T(8,128)(2,1)S(1)}, bf16[88,1024]{1,0:T(8,128)(2,1)S(1)}, u32[]{:S(2)}, u32[]{:S(2)}) collective-permute-start(bf16[88,1024]{1,0:T(8,128)(2,1)S(1)} %get-tuple-element.46.refs_0_), channel_id=1, source_target_pairs={{0,64},{2,66},{4,68},{6,70},{8,72},{10,74},{12,76},{14,78},{16,80}... | collective-permute-start | bytes 540680 | tf_op jit(solution)/shard_map/ppermute | solution.py:390
  14.6 40.5 %collective-permute-start.6 = (bf16[320,5120]{1,0:T(8,128)(2,1)}, bf16[320,5120]{1,0:T(8,128)(2,1)S(1)}, u32[]{:S(2)}, u32[]{:S(2)}) collective-permute-start(bf16[320,5120]{1,0:T(8,128)(2,1)} %bitcast.6), channel_id=1, source_target_pairs={{0,2},{1,3},{2,0},{3,1},{4,6},{5,7},{6,4},{7,5},{8,10},{9,11},{10,... | collective-permute-start | bytes 9830408 | tf_op jit(solution)/shard_map/ppermute | solution.py:399
  25.2 28.3 %collective-permute-start.5 = (bf16[80,1280]{1,0:T(8,128)(2,1)}, bf16[80,1280]{1,0:T(8,128)(2,1)S(1)}, u32[]{:S(2)}, u32[]{:S(2)}) collective-permute-start(bf16[80,1280]{1,0:T(8,128)(2,1)} %refs_0_), channel_id=1, source_target_pairs={{0,1},{1,0},{2,3},{3,2},{4,5},{5,4},{6,7},{7,6},{8,9},{9,8},{10,11... | collective-permute-start | bytes 614408 | tf_op jit(solution)/shard_map/ppermute | solution.py:399
  28.1 26.9 %collective-permute-start.8 = (bf16[88,1024]{1,0:T(8,128)(2,1)S(1)}, bf16[88,1024]{1,0:T(8,128)(2,1)S(1)}, u32[]{:S(2)}, u32[]{:S(2)}) collective-permute-start(bf16[88,1024]{1,0:T(8,128)(2,1)S(1)} %get-tuple-element.46.refs_0_), channel_id=1, source_target_pairs={{0,160},{2,226},{4,164},{6,230},{8,168},{10,234},{12,172},{14,238}... | collective-permute-start | bytes 540680 | tf_op jit(solution)/shard_map/ppermute | solution.py:390
  28.1 26.9 %collective-permute-start.9 = (bf16[88,1024]{1,0:T(8,128)(2,1)S(1)}, bf16[88,1024]{1,0:T(8,128)(2,1)S(1)}, u32[]{:S(2)}, u32[]{:S(2)}) collective-permute-start(bf16[88,1024]{1,0:T(8,128)(2,1)S(1)} %get-tuple-element.46.refs_0_), channel_id=1, source_target_pairs={{0,224},{2,162},{4,228},{6,166},{8,232},{10,170},{12,236},{14,174}... | collective-permute-start | bytes 540680 | tf_op jit(solution)/shard_map/ppermute | solution.py:390
  31.2 23.8 %collective-permute-start.7 = (f32[1,320]{1,0:T(1,128)S(1)}, f32[1,320]{1,0:T(1,128)S(1)}, u32[]{:S(2)}, u32[]{:S(2)}) collective-permute-start(f32[1,320]{1,0:T(1,128)S(1)} %broadcast_in_dim.13.refs_12_), channel_id=1, source_target_pairs={{0,2},{1,3},{2,0},{3,1},{4,6},{5,7},{6,4},{7,5},{8,10},{9,11},{10,... | collective-permute-start | bytes 3848 | tf_op jit(solution)/shard_map/ppermute | solution.py:399
  53.5 0.9 copy-start.1
  55.0 41.7 %copy-start.2 = (f32[1280]{0:T(1024)S(1)}, f32[1280]{0:T(1024)}, u32[]{:S(2)}) copy-start(f32[1280]{0:T(1024)} %param.14) | copy-start | bytes 15364
  55.0 41.7 %copy-start.3 = (f32[1280]{0:T(1024)S(1)}, f32[1280]{0:T(1024)}, u32[]{:S(2)}) copy-start(f32[1280]{0:T(1024)} %param.15) | copy-start | bytes 15364
  55.0 10.3 %collective-permute-start.12 = (bf16[160,1280]{1,0:T(8,128)(2,1)S(1)}, bf16[160,1280]{1,0:T(8,128)(2,1)S(1)}, u32[]{:S(2)}, u32[]{:S(2)}) collective-permute-start(bf16[160,1280]{1,0:T(8,128)(2,1)S(1)} %both.1.refs_0_), channel_id=1, source_target_pairs={{0,4},{1,5},{2,6},{3,7},{4,8},{5,9},{6,10},{7,11},{8,12},{9,13},{1... | collective-permute-start | bytes 1228808 | tf_op jit(solution)/shard_map/ppermute | solution.py:399
  55.3 15.6 %collective-permute-start.13 = (bf16[160,1280]{1,0:T(8,128)(2,1)S(1)}, bf16[160,1280]{1,0:T(8,128)(2,1)S(1)}, u32[]{:S(2)}, u32[]{:S(2)}) collective-permute-start(bf16[160,1280]{1,0:T(8,128)(2,1)S(1)} %both.1.refs_0_), channel_id=1, source_target_pairs={{0,12},{1,13},{2,14},{3,15},{4,0},{5,1},{6,2},{7,3},{8,4},{9,5},{1... | collective-permute-start | bytes 1228808 | tf_op jit(solution)/shard_map/ppermute | solution.py:399
  56.6 14.3 %collective-permute-start.14 = (bf16[160,1280]{1,0:T(8,128)(2,1)S(1)}, bf16[160,1280]{1,0:T(8,128)(2,1)S(1)}, u32[]{:S(2)}, u32[]{:S(2)}) collective-permute-start(bf16[160,1280]{1,0:T(8,128)(2,1)S(1)} %both.1.refs_0_), channel_id=1, source_target_pairs={{0,8},{1,9},{2,10},{3,11},{4,12},{5,13},{6,14},{7,15},{8,0},{9,1},... | collective-permute-start | bytes 1228808 | tf_op jit(solution)/shard_map/ppermute | solution.py:399
  57.7 14.1 %collective-permute-start.4 = (bf16[88,1024]{1,0:T(8,128)(2,1)S(1)}, bf16[88,1024]{1,0:T(8,128)(2,1)S(1)}, u32[]{:S(2)}, u32[]{:S(2)}) collective-permute-start(bf16[88,1024]{1,0:T(8,128)(2,1)S(1)} %get-tuple-element.42), channel_id=1, source_target_pairs={{0,64},{2,66},{4,68},{6,70},{8,72},{10,74},{12,76},{14,78},{16,80}... | collective-permute-start | bytes 540680 | tf_op jit(solution)/shard_map/ppermute | solution.py:390
  65.3 11.0 %collective-permute-start.10 = (bf16[88,1024]{1,0:T(8,128)(2,1)S(1)}, bf16[88,1024]{1,0:T(8,128)(2,1)S(1)}, u32[]{:S(2)}, u32[]{:S(2)}) collective-permute-start(bf16[88,1024]{1,0:T(8,128)(2,1)S(1)} %get-tuple-element.53), channel_id=1, source_target_pairs={{0,160},{2,226},{4,164},{6,230},{8,168},{10,234},{12,172},{14,238}... | collective-permute-start | bytes 540680 | tf_op jit(solution)/shard_map/ppermute | solution.py:390
  65.4 10.9 %collective-permute-start.11 = (bf16[88,1024]{1,0:T(8,128)(2,1)S(1)}, bf16[88,1024]{1,0:T(8,128)(2,1)S(1)}, u32[]{:S(2)}, u32[]{:S(2)}) collective-permute-start(bf16[88,1024]{1,0:T(8,128)(2,1)S(1)} %get-tuple-element.54), channel_id=1, source_target_pairs={{0,224},{2,162},{4,228},{6,166},{8,232},{10,170},{12,236},{14,174}... | collective-permute-start | bytes 540680 | tf_op jit(solution)/shard_map/ppermute | solution.py:390
  76.2 16.5 %collective-permute-start.19 = (bf16[640,1280]{1,0:T(8,128)(2,1)S(1)}, bf16[640,1280]{1,0:T(8,128)(2,1)S(1)}, u32[]{:S(2)}, u32[]{:S(2)}) collective-permute-start(bf16[640,1280]{1,0:T(8,128)(2,1)S(1)} %assemble.1.refs_0_), channel_id=1, source_target_pairs={{0,2},{1,3},{2,0},{3,1},{4,6},{5,7},{6,4},{7,5},{8,10},{9,11},{10,... | collective-permute-start | bytes 4915208 | tf_op jit(solution)/shard_map/ppermute | solution.py:399
  76.5 3.4 %collective-permute-start.15 = (bf16[80,512]{1,0:T(8,128)(2,1)S(1)}, bf16[80,512]{1,0:T(8,128)(2,1)S(1)}, u32[]{:S(2)}, u32[]{:S(2)}) collective-permute-start(bf16[80,512]{1,0:T(8,128)(2,1)S(1)} %get-tuple-element.65), channel_id=1, source_target_pairs={{0,2},{1,3},{2,0},{3,1},{4,6},{5,7},{6,4},{7,5},{8,10},{9,11},{10,... | collective-permute-start | bytes 245768 | tf_op jit(solution)/shard_map/ppermute | solution.py:399
  80.1 8.3 %collective-permute-start.16 = (bf16[160,512]{1,0:T(8,128)(2,1)S(1)}, bf16[160,512]{1,0:T(8,128)(2,1)S(1)}, u32[]{:S(2)}, u32[]{:S(2)}) collective-permute-start(bf16[160,512]{1,0:T(8,128)(2,1)S(1)} %pair.1.refs_0_), channel_id=1, source_target_pairs={{0,1},{1,0},{2,3},{3,2},{4,5},{5,4},{6,7},{7,6},{8,9},{9,8},{10,11... | collective-permute-start | bytes 491528 | tf_op jit(solution)/shard_map/ppermute | solution.py:399
  82.7 8.6 %collective-permute-start.20 = (bf16[160,512]{1,0:T(8,128)(2,1)S(1)}, bf16[160,512]{1,0:T(8,128)(2,1)S(1)}, u32[]{:S(2)}, u32[]{:S(2)}) collective-permute-start(bf16[160,512]{1,0:T(8,128)(2,1)S(1)} %pair.1.refs_0_), channel_id=1, source_target_pairs={{0,12},{1,13},{2,14},{3,15},{4,0},{5,1},{6,2},{7,3},{8,4},{9,5},{1... | collective-permute-start | bytes 491528 | tf_op jit(solution)/shard_map/ppermute | solution.py:399
  84.5 16.6 %collective-permute-start.17 = (bf16[160,512]{1,0:T(8,128)(2,1)S(1)}, bf16[160,512]{1,0:T(8,128)(2,1)S(1)}, u32[]{:S(2)}, u32[]{:S(2)}) collective-permute-start(bf16[160,512]{1,0:T(8,128)(2,1)S(1)} %pair.1.refs_0_), channel_id=1, source_target_pairs={{0,4},{1,5},{2,6},{3,7},{4,8},{5,9},{6,10},{7,11},{8,12},{9,13},{1... | collective-permute-start | bytes 491528 | tf_op jit(solution)/shard_map/ppermute | solution.py:399
  85.4 15.7 %collective-permute-start.18 = (bf16[160,512]{1,0:T(8,128)(2,1)S(1)}, bf16[160,512]{1,0:T(8,128)(2,1)S(1)}, u32[]{:S(2)}, u32[]{:S(2)}) collective-permute-start(bf16[160,512]{1,0:T(8,128)(2,1)S(1)} %pair.1.refs_0_), channel_id=1, source_target_pairs={{0,5},{1,4},{2,7},{3,6},{4,9},{5,8},{6,11},{7,10},{8,13},{9,12},{1... | collective-permute-start | bytes 491528 | tf_op jit(solution)/shard_map/ppermute | solution.py:399
  88.4 12.8 %collective-permute-start.21 = (bf16[160,512]{1,0:T(8,128)(2,1)S(1)}, bf16[160,512]{1,0:T(8,128)(2,1)S(1)}, u32[]{:S(2)}, u32[]{:S(2)}) collective-permute-start(bf16[160,512]{1,0:T(8,128)(2,1)S(1)} %pair.1.refs_0_), channel_id=1, source_target_pairs={{0,13},{1,12},{2,15},{3,14},{4,1},{5,0},{6,3},{7,2},{8,5},{9,4},{1... | collective-permute-start | bytes 491528 | tf_op jit(solution)/shard_map/ppermute | solution.py:399
  91.4 9.9 %collective-permute-start.22 = (bf16[160,512]{1,0:T(8,128)(2,1)S(1)}, bf16[160,512]{1,0:T(8,128)(2,1)S(1)}, u32[]{:S(2)}, u32[]{:S(2)}) collective-permute-start(bf16[160,512]{1,0:T(8,128)(2,1)S(1)} %pair.1.refs_0_), channel_id=1, source_target_pairs={{0,8},{1,9},{2,10},{3,11},{4,12},{5,13},{6,14},{7,15},{8,0},{9,1},... | collective-permute-start | bytes 491528 | tf_op jit(solution)/shard_map/ppermute | solution.py:399
  92.7 12.9 %collective-permute-start.23 = (bf16[160,512]{1,0:T(8,128)(2,1)S(1)}, bf16[160,512]{1,0:T(8,128)(2,1)S(1)}, u32[]{:S(2)}, u32[]{:S(2)}) collective-permute-start(bf16[160,512]{1,0:T(8,128)(2,1)S(1)} %pair.1.refs_0_), channel_id=1, source_target_pairs={{0,9},{1,8},{2,11},{3,10},{4,13},{5,12},{6,15},{7,14},{8,1},{9,0},... | collective-permute-start | bytes 491528 | tf_op jit(solution)/shard_map/ppermute | solution.py:399
  96.7 8.9 %copy-start = (bf16[5120,320]{0,1:T(8,128)(2,1)S(1)}, bf16[5120,320]{0,1:T(8,128)(2,1)}, u32[]{:S(2)}) copy-start(bf16[5120,320]{0,1:T(8,128)(2,1)} %param.16) | copy-start | bytes 9830404
  110.0 2.7 %collective-permute-start.24 = (bf16[320,128]{1,0:T(8,128)(2,1)S(1)}, bf16[320,128]{1,0:T(8,128)(2,1)S(1)}, u32[]{:S(2)}, u32[]{:S(2)}) collective-permute-start(bf16[320,128]{1,0:T(8,128)(2,1)S(1)} %get-tuple-element.72), channel_id=1, source_target_pairs={{0,2},{1,3},{2,0},{3,1},{4,6},{5,7},{6,4},{7,5},{8,10},{9,11},{10,... | collective-permute-start | bytes 245768 | tf_op jit(solution)/shard_map/ppermute | solution.py:399
